TPU v7x, 256 devices: a whole 4x4x8 slice. The times are simulated.
256 devices in a mesh: section: 8 (over x, z_lo), dp: 32 (over z_hi, y, core).
Axes of the slice: x: 4, y: 4, z: 8 (z_hi: 4, z_lo: 2; z = z_hi * 2 + z_lo), core: 2. Of those that a mesh axis runs over, the one named last changes fastest.
Arguments:
- enc_in: bfloat16 [512, 16, 16, 320], P(('dp', 'section')), parts along dimension 0, may hold values from -6 to 6
- dec_in: bfloat16 [512, 16, 16, 320], P(('dp', 'section')), parts along dimension 0, may hold values from -6 to 6
- fresh: bfloat16 [64, 16, 16, 320], P('dp'), parts along dimension 0, may hold values from -6 to 6
- skip_queue: bfloat16 [1024, 16, 16, 320], P(('dp', 'section')), parts along dimension 0, may hold values from -6 to 6
- enc_weight: bfloat16 [8, 3, 3, 320, 320], P('section'), may hold values from -0.109375 to 0.109375
- enc_bias: float32 [8, 320], P('section'), may hold values from -2 to 2
- enc_gain: float32 [8, 320], P('section'), may hold values from 0.25 to 1.75
- enc_beta: float32 [8, 320], P('section'), may hold values from -2 to 2
- dec_weight: bfloat16 [8, 3, 3, 640, 320], P('section'), may hold values from -0.078125 to 0.078125
- dec_bias: float32 [8, 320], P('section'), may hold values from -2 to 2
- dec_gain: float32 [8, 640], P('section'), may hold values from 0.25 to 1.75
- dec_beta: float32 [8, 640], P('section'), may hold values from -2 to 2
Outputs:
- encoded: bfloat16 [1024, 16, 16, 320], P(('dp', 'section')), parts along dimension 0
- decoded: bfloat16 [1024, 16, 16, 320], P(('dp', 'section')), parts along dimension 0
- queued: bfloat16 [1024, 16, 16, 320], P(('dp', 'section')), parts along dimension 0
There are 32 independent parts, one for each index of `dp`. A program takes and returns all parts, laid end to end along the dimension named above; an argument that names none is the same for every part. Nothing has to cross between parts.
All inputs are finite; a program needn't handle non-finite values.
Results may differ from a plain program's by a relative error of at most 0.0048.
Values may be sent and summed in bfloat16 or wider, within the bound.
No kernel may reach another device: no remote copies, remote signals or barrier semaphores. Data moves between devices by JAX's collectives and lax.ppermute only.
A program may use at most 64 MiB of HBM per device.

v0:
```python
import jax
import jax.numpy as jnp
from jax import lax
from jax.sharding import PartitionSpec as P

GROUPS = 32
TICKS = 2


def from_partner(value, axis, apart):
    mask = 2**apart
    pairs = [(source, source ^ mask) for source in range(lax.axis_size(axis))]
    return lax.ppermute(value, axis, pairs)


def from_behind(value, axis, steps):
    count = lax.axis_size(axis)
    pairs = [(source, (source + steps) % count) for source in range(count)]
    return lax.ppermute(value, axis, pairs)


def norm_silu(values, norm_gain, norm_beta):
    layout = values.shape
    grouped = values.reshape(layout[:3] + (GROUPS, layout[3] // GROUPS))
    average = jnp.mean(grouped, axis=(1, 2, 4), keepdims=True)
    centred = grouped - average
    variance = jnp.mean(centred * centred, axis=(1, 2, 4), keepdims=True)
    normed = (centred * lax.rsqrt(variance + 1e-05)).reshape(layout)
    return jax.nn.silu(normed * norm_gain + norm_beta).astype(jnp.bfloat16)


def convolve(inputs, kernel):
    return lax.conv_general_dilated(
        inputs,
        kernel,
        (1, 1),
        "SAME",
        dimension_numbers=("NHWC", "HWIO", "NHWC"),
        preferred_element_type=jnp.float32,
    )


def encode(current, kernel, bias_row, norm_gain, norm_beta):
    widened = current.astype(jnp.float32)
    hidden = norm_silu(widened, norm_gain, norm_beta)
    return (widened + convolve(hidden, kernel) + bias_row).astype(jnp.bfloat16)


def decode(current, skipped, kernel, bias_row, norm_gain, norm_beta):
    joined = jnp.concatenate([current, skipped], axis=3).astype(jnp.float32)
    hidden = norm_silu(joined, norm_gain, norm_beta)
    return (current.astype(jnp.float32) + convolve(hidden, kernel) + bias_row).astype(jnp.bfloat16)


def shards(
    enc_in,
    dec_in,
    fresh,
    skip_queue,
    enc_weight,
    enc_bias,
    enc_gain,
    enc_beta,
    dec_weight,
    dec_bias,
    dec_gain,
    dec_beta,
):
    place = lax.axis_index("section")
    leading = place == 0
    sections = lax.axis_size("section")
    bit_count = sections.bit_length() - 1
    images = enc_in.shape[0]
    map_dims = enc_in.shape[1:]
    queue = skip_queue.reshape((TICKS, images) + map_dims)
    arrivals = fresh.reshape((TICKS - 1, images) + map_dims)
    bit_list = list(range(bit_count))
    enc_now = enc_in
    dec_now = dec_in
    enc_list, dec_list, queue_list = ([], [], [])
    previous = None
    for turn_index in range(TICKS):
        skipped = queue[turn_index]
        if turn_index > 0:
            skipped = jnp.where(leading, previous, skipped)
        enc_out = encode(enc_now, enc_weight[0], enc_bias[0], enc_gain[0], enc_beta[0])
        values = enc_out
        for bit_index in bit_list:
            values = from_partner(values, "section", bit_index)
        dec_out = decode(dec_now, skipped, dec_weight[0], dec_bias[0], dec_gain[0], dec_beta[0])
        previous = values
        enc_list.append(enc_out)
        dec_list.append(dec_out)
        queue_list.append(values)
        if turn_index + 1 < TICKS:
            moved_enc, moved_dec = from_behind((enc_out, dec_out), "section", 1)
            dec_now = jnp.where(leading, moved_enc, moved_dec)
            enc_now = jnp.where(leading, arrivals[turn_index], moved_enc)
    encoded = jnp.concatenate(enc_list, axis=0)
    decoded = jnp.concatenate(dec_list, axis=0)
    queued = jnp.concatenate(queue_list, axis=0)
    return (encoded, decoded, queued)


def solution(mesh):
    in_specs = (
        P(("dp", "section"), None, None, None),
        P(("dp", "section"), None, None, None),
        P("dp", None, None, None),
        P(("dp", "section"), None, None, None),
        P("section", None, None, None, None),
        P("section", None),
        P("section", None),
        P("section", None),
        P("section", None, None, None, None),
        P("section", None),
        P("section", None),
        P("section", None),
    )
    out_specs = (
        P(("dp", "section"), None, None, None),
        P(("dp", "section"), None, None, None),
        P(("dp", "section"), None, None, None),
    )
    return jax.shard_map(shards, mesh=mesh, in_specs=in_specs, out_specs=out_specs, check_vma=False)
```

profile of v0, /device:TPU:82, one launch (start us, length us, event | category | flops | bytes accessed | tf_op | source)
XLA Modules:
  0.0 128.3 jit_solution(18057532104973385953)
XLA Ops:
  0.6 1.2 convert_reduce_fusion.1
  2.3 1.1 fusion.55
  3.8 0.7 reduce.8
  4.5 0.7 reduce.9
  5.3 1.3 %fusion.76 = bf16[16,2,16,320]{3,0,2,1:T(8,128)(2,1)S(1)} fusion(f32[320]{0:T(512)S(1)} %reduce.9, f32[320]{0:T(512)S(1)} %reduce.8, f32[2,320]{1,0:T(2,128)S(1)} %mul.114, f32[2,320]{1,0:T(2,128)S(1)} %sub.63, bf16[2,16,16,320]{3,2,1,0:T(8,128)(2,1)} %param.12), kind=kLoop, calls=%fused_computation.86 | loop fusion | flops 1638400 | bytes 663040 | tf_op jit(solution)/shard_map/convert_element_type | solution.py:29
  6.8 2.5 %fusion.19 = f32[16,16,3,320]{3,1,2,0:T(8,128)S(1)} fusion(bf16[1,3,3,320,320]{4,3,2,1,0:T(8,128)(2,1)S(1)} %copy-done, bf16[16,2,8,5,320]{4,0,3,2,1:T(8,128)(2,1)S(1)} %fusion.36, pred[16,3]{0,1:T(4,128)(4,1)S(1)} %copy-done.15), kind=kOutput, calls=%fused_computation.26 | convolution fusion | flops 1356840960 | bytes 3645488 | tf_op jit(solution)/shard_map/conv_general_dilated | solution.py:33
  9.4 1.4 %copy.21 = f32[16,16,3,320]{3,0,2,1:T(8,128)} copy(f32[16,16,3,320]{3,1,2,0:T(8,128)S(1)} %fusion.19) | data formatting | bytes 1966080 | tf_op jit(solution)/shard_map/conv_general_dilated | solution.py:33
  10.8 2.0 %fusion.65 = bf16[2,16,16,320]{3,1,2,0:T(8,128)(2,1)} fusion(f32[16,2,24,320]{3,0,2,1:T(8,128)} %bitcast.101, f32[320]{0:T(512)S(1)} %reduce.10, bf16[2,16,16,320]{3,2,1,0:T(8,128)(2,1)S(1)} %copy-done.5), kind=kLoop, calls=%fused_computation.68 | loop fusion | flops 655360 | bytes 1312000 | tf_op jit(solution)/shard_map/convert_element_type | solution.py:46
  12.8 1.9 %collective-permute-start = (bf16[2,16,16,320]{3,1,2,0:T(8,128)(2,1)}, bf16[2,16,16,320]{3,1,2,0:T(8,128)(2,1)}, u32[]{:S(2)}, u32[]{:S(2)}) collective-permute-start(bf16[2,16,16,320]{3,1,2,0:T(8,128)(2,1)} %fusion.65), channel_id=1, source_target_pairs={{0,32},{32,64},{64,96},{96,128},{128,160},{160,192},{192,224},{224... | collective-permute-start | bytes 983048 | tf_op jit(solution)/shard_map/ppermute | solution.py:19
  14.7 1.0 collective-permute-start.2
  15.7 1.9 %fusion.78 = (bf16[2,16,16,320]{3,2,1,0:T(8,128)(2,1)S(1)}, bf16[2,16,16,320]{3,2,1,0:T(8,128)(2,1)}) fusion(bf16[4,16,16,320]{3,2,1,0:T(8,128)(2,1)} %param.15), kind=kLoop, calls=%fused_computation.99 | loop fusion | bytes 1310720 | tf_op jit(solution)/shard_map/slice | solution.py:83
  17.7 3.7 %concatenate.27 = bf16[2,16,16,16,20]{4,3,2,1,0:T(8,128)(2,1)} reshape(bf16[2,16,16,320]{3,2,1,0:T(8,128)(2,1)S(1)} %get-tuple-element.8) | data formatting | bytes 655360 | tf_op jit(solution)/shard_map/concatenate | solution.py:50
  21.4 3.7 %concatenate.26 = bf16[2,16,16,16,20]{4,3,2,1,0:T(8,128)(2,1)} reshape(bf16[2,16,16,320]{3,2,1,0:T(8,128)(2,1)S(1)} %copy-done.6) | data formatting | bytes 655360 | tf_op jit(solution)/shard_map/concatenate | solution.py:50
  25.1 3.6 %fusion.35 = f32[2,32]{1,0:T(2,128)S(1)} fusion(bf16[2,16,16,16,20]{4,3,2,1,0:T(8,128)(2,1)} %concatenate.27, bf16[2,16,16,16,20]{4,3,2,1,0:T(8,128)(2,1)} %concatenate.26), kind=kLoop, calls=%fused_computation.32 | loop fusion | flops 1638336 | bytes 655616 | tf_op jit(solution)/shard_map/reduce_sum | solution.py:25
  28.7 4.4 %maximum_convert_fusion = f32[2,16,16,32,20]{4,3,2,1,0:T(8,128)} fusion(bf16[2,16,16,16,20]{4,3,2,1,0:T(8,128)(2,1)S(1)} %copy-done.2, bf16[2,16,16,16,20]{4,3,2,1,0:T(8,128)(2,1)S(1)} %copy-done.4), kind=kLoop, calls=%fused_computation.2 | loop fusion | flops 1310720 | bytes 1966080 | tf_op jit(solution)/shard_map/convert_element_type | solution.py:50
  33.1 2.0 %multiply_reduce_fusion.1 = f32[2,32]{1,0:T(2,128)S(1)} fusion(f32[2,32]{1,0:T(2,128)S(1)} %broadcast_multiply_fusion.1, bf16[2,16,16,16,20]{4,3,2,1,0:T(8,128)(2,1)S(1)} %copy-done.2, bf16[2,16,16,16,20]{4,3,2,1,0:T(8,128)(2,1)S(1)} %copy-done.4), kind=kLoop, calls=%fused_computation.1 | loop fusion | flops 2293696 | bytes 655872 | tf_op jit(solution)/shard_map/reduce_sum | solution.py:27
  35.5 7.7 %reshape.125 = f32[2,16,16,640]{3,2,1,0:T(8,128)S(1)} reshape(f32[2,16,16,32,20]{4,3,2,1,0:T(8,128)} %maximum_convert_fusion) | data formatting | bytes 2621440 | tf_op jit(solution)/shard_map/convert_element_type | solution.py:50
  43.2 0.7 reduce.12
  43.9 0.4 fusion.74
  44.8 1.8 %copy-done.13 = bf16[1,3,3,640,320]{3,4,2,1,0:T(8,128)(2,1)S(1)} copy-done((bf16[1,3,3,640,320]{3,4,2,1,0:T(8,128)(2,1)S(1)}, bf16[1,3,3,640,320]{3,4,2,1,0:T(8,128)(2,1)}, u32[]{:S(2)}) %copy-start.13) | copy-done | bytes 3686424
  46.6 4.8 %fusion.25 = f32[16,16,3,320]{3,1,2,0:T(8,128)S(1)} fusion(bf16[1,3,3,640,320]{3,4,2,1,0:T(8,128)(2,1)S(1)} %copy-done.13, bf16[16,2,8,5,640]{4,0,3,2,1:T(8,128)(2,1)S(1)} %fusion.13, pred[16,3]{0,1:T(4,128)(4,1)S(1)} %copy-done.16), kind=kOutput, calls=%fused_computation.28 | convolution fusion | flops 2713436160 | bytes 6307888 | tf_op jit(solution)/shard_map/conv_general_dilated | solution.py:33
  52.1 1.9 %fusion.73 = bf16[2,16,16,320]{3,1,2,0:T(8,128)(2,1)} fusion(f32[16,2,24,320]{3,0,2,1:T(8,128)S(1)} %bitcast.99, bf16[2,16,16,320]{3,2,1,0:T(8,128)(2,1)} %param.13, f32[320]{0:T(512)S(1)} %reduce.13), kind=kLoop, calls=%fused_computation.78 | loop fusion | flops 655360 | bytes 1312000 | tf_op jit(solution)/shard_map/convert_element_type | solution.py:52
  54.0 1.0 collective-permute-start.1
  55.0 1.3 convert_reduce_fusion
  57.8 0.5 collective-permute-start.3
  58.3 2.5 %fusion.22 = f32[16,16,3,320]{3,1,2,0:T(8,128)S(1)} fusion(bf16[1,3,3,320,320]{4,3,2,1,0:T(8,128)(2,1)S(1)} %copy-done, bf16[16,2,8,5,320]{4,0,3,2,1:T(8,128)(2,1)S(1)} %fusion.37, pred[16,3]{0,1:T(4,128)(4,1)S(1)} %copy-done.16), kind=kOutput, calls=%fused_computation.27 | convolution fusion | flops 1356840960 | bytes 3645488 | tf_op jit(solution)/shard_map/conv_general_dilated | solution.py:33
  60.8 0.4 copy.24
  61.3 2.2 %collective-permute-start.5 = (bf16[2,16,16,320]{3,1,2,0:T(8,128)(2,1)S(1)}, bf16[2,16,16,320]{3,1,2,0:T(8,128)(2,1)}, u32[]{:S(2)}, u32[]{:S(2)}) collective-permute-start(bf16[2,16,16,320]{3,1,2,0:T(8,128)(2,1)S(1)} %fusion.67), channel_id=1, source_target_pairs={{0,32},{32,0},{64,96},{96,64},{128,160},{160,128},{192,224},{224,1... | collective-permute-start | bytes 983048 | tf_op jit(solution)/shard_map/ppermute | solution.py:13
  63.5 10.5 %collective-permute-done.3 = bf16[2,16,16,320]{3,1,2,0:T(8,128)(2,1)} collective-permute-done((bf16[2,16,16,320]{3,1,2,0:T(8,128)(2,1)}, bf16[2,16,16,320]{3,1,2,0:T(8,128)(2,1)}, u32[]{:S(2)}, u32[]{:S(2)}) %collective-permute-start.3) | collective-permute-done | bytes 327712 | tf_op jit(solution)/shard_map/ppermute | solution.py:13
  74.0 1.4 %collective-permute-start.4 = (bf16[2,16,16,320]{3,1,2,0:T(8,128)(2,1)}, bf16[2,16,16,320]{3,1,2,0:T(8,128)(2,1)S(1)}, u32[]{:S(2)}, u32[]{:S(2)}) collective-permute-start(bf16[2,16,16,320]{3,1,2,0:T(8,128)(2,1)} %collective-permute-done.3), channel_id=1, source_target_pairs={{0,128},{32,160},{64,192},{96,224},{128,0},{160,32},{192,64},{224,... | collective-permute-start | bytes 983048 | tf_op jit(solution)/shard_map/ppermute | solution.py:13
  75.3 1.0 broadcast_select_fusion
  76.4 2.7 %concatenate.29 = bf16[2,16,16,16,20]{4,3,1,2,0:T(8,128)(2,1)S(1)} reshape(bf16[2,16,16,320]{3,1,2,0:T(8,128)(2,1)S(1)} %broadcast_select_fusion) | data formatting | bytes 655360 | tf_op jit(solution)/shard_map/concatenate | solution.py:50
  79.1 1.2 pad_maximum_fusion.1
  80.3 1.0 copy.35
  81.5 6.1 %collective-permute-done.4 = bf16[2,16,16,320]{3,1,2,0:T(8,128)(2,1)S(1)} collective-permute-done((bf16[2,16,16,320]{3,1,2,0:T(8,128)(2,1)}, bf16[2,16,16,320]{3,1,2,0:T(8,128)(2,1)S(1)}, u32[]{:S(2)}, u32[]{:S(2)}) %collective-permute-start.4) | collective-permute-done | bytes 327712 | tf_op jit(solution)/shard_map/ppermute | solution.py:13
  87.8 3.8 %concatenate.30 = bf16[2,16,16,16,20]{4,3,1,2,0:T(8,128)(2,1)} reshape(bf16[2,16,16,320]{3,1,2,0:T(8,128)(2,1)S(1)} %copy_select_fusion) | data formatting | bytes 655360 | tf_op jit(solution)/shard_map/concatenate | solution.py:50
  91.5 2.7 %fusion.6 = f32[2,32]{1,0:T(2,128)S(1)} fusion(bf16[2,16,16,16,20]{4,3,1,2,0:T(8,128)(2,1)} %concatenate.30, bf16[2,16,16,16,20]{4,3,1,2,0:T(8,128)(2,1)S(1)} %concatenate.29), kind=kLoop, calls=%fused_computation.12 | loop fusion | flops 1966016 | bytes 655616 | tf_op jit(solution)/shard_map/reduce_sum | solution.py:25
  94.2 3.8 %copy_convert_fusion = f32[2,16,16,32,20]{4,3,2,1,0:T(8,128)} fusion(bf16[2,16,16,16,20]{4,3,1,2,0:T(8,128)(2,1)S(1)} %copy-done.3, bf16[2,16,16,16,20]{4,3,1,2,0:T(8,128)(2,1)S(1)} %concatenate.29), kind=kLoop, calls=%fused_computation.4 | loop fusion | flops 1638400 | bytes 1966080 | tf_op jit(solution)/shard_map/convert_element_type | solution.py:50
  98.1 2.0 %multiply_reduce_fusion = f32[2,32]{1,0:T(2,128)S(1)} fusion(f32[2,32]{1,0:T(2,128)S(1)} %broadcast_multiply_fusion, bf16[2,16,16,16,20]{4,3,1,2,0:T(8,128)(2,1)S(1)} %copy-done.3, bf16[2,16,16,16,20]{4,3,1,2,0:T(8,128)(2,1)S(1)} %concatenate.29), kind=kLoop, calls=%fused_computation | loop fusion | flops 2621376 | bytes 655872 | tf_op jit(solution)/shard_map/reduce_sum | solution.py:27
  100.4 7.7 %reshape.126 = f32[2,16,16,640]{3,2,1,0:T(8,128)S(1)} reshape(f32[2,16,16,32,20]{4,3,2,1,0:T(8,128)} %copy_convert_fusion) | data formatting | bytes 2621440 | tf_op jit(solution)/shard_map/convert_element_type | solution.py:50
  108.2 0.4 fusion.75
  109.0 1.8 %copy-done.14 = bf16[1,3,3,640,320]{3,4,2,1,0:T(8,128)(2,1)S(1)} copy-done((bf16[1,3,3,640,320]{3,4,2,1,0:T(8,128)(2,1)S(1)}, bf16[1,3,3,640,320]{3,4,2,1,0:T(8,128)(2,1)}, u32[]{:S(2)}) %copy-start.14) | copy-done | bytes 3686424
  110.9 4.8 %fusion.30 = f32[16,16,3,320]{3,1,2,0:T(8,128)S(1)} fusion(bf16[1,3,3,640,320]{3,4,2,1,0:T(8,128)(2,1)S(1)} %copy-done.14, bf16[16,2,8,5,640]{4,0,3,2,1:T(8,128)(2,1)S(1)} %fusion.14, pred[16,3]{0,1:T(4,128)(4,1)S(1)} %copy-done.16), kind=kOutput, calls=%fused_computation.29 | convolution fusion | flops 2713436160 | bytes 6307888 | tf_op jit(solution)/shard_map/conv_general_dilated | solution.py:33
  116.0 1.5 %collective-permute-start.7 = (bf16[2,16,16,320]{3,1,2,0:T(8,128)(2,1)}, bf16[2,16,16,320]{3,1,2,0:T(8,128)(2,1)S(1)}, u32[]{:S(2)}, u32[]{:S(2)}) collective-permute-start(bf16[2,16,16,320]{3,1,2,0:T(8,128)(2,1)} %collective-permute-done.6), channel_id=1, source_target_pairs={{0,128},{32,160},{64,192},{96,224},{128,0},{160,32},{192,64},{224,... | collective-permute-start | bytes 983048 | tf_op jit(solution)/shard_map/ppermute | solution.py:13
  117.6 1.3 %pad_maximum_fusion.2 = bf16[4,16,16,320]{3,1,2,0:T(8,128)(2,1)S(1)} fusion(bf16[2,16,16,320]{3,1,2,0:T(8,128)(2,1)S(1)} %fusion.70, bf16[2,16,16,320]{3,1,2,0:T(8,128)(2,1)} %fusion.73), kind=kLoop, calls=%fused_computation.82 | loop fusion | flops 327680 | bytes 1310720 | tf_op jit(solution)/shard_map/concatenate | solution.py:100
  118.9 1.0 copy.36
  120.0 7.1 %collective-permute-done.7 = bf16[2,16,16,320]{3,1,2,0:T(8,128)(2,1)S(1)} collective-permute-done((bf16[2,16,16,320]{3,1,2,0:T(8,128)(2,1)}, bf16[2,16,16,320]{3,1,2,0:T(8,128)(2,1)S(1)}, u32[]{:S(2)}, u32[]{:S(2)}) %collective-permute-start.7) | collective-permute-done | bytes 327712 | tf_op jit(solution)/shard_map/ppermute | solution.py:13
  127.2 1.0 copy.37
  (95 shorter events, 5.7 us)
Async XLA Ops:
  0.6 6.2 %copy-start = (bf16[1,3,3,320,320]{4,3,2,1,0:T(8,128)(2,1)S(1)}, bf16[1,3,3,320,320]{4,3,2,1,0:T(8,128)(2,1)}, u32[]{:S(2)}) copy-start(bf16[1,3,3,320,320]{4,3,2,1,0:T(8,128)(2,1)} %param.16) | copy-start | bytes 5529604
  5.2 1.5 %copy-start.8 = (f32[320]{0:T(512)}, f32[320]{0:T(512)S(1)}, u32[]{:S(2)}) copy-start(f32[320]{0:T(512)S(1)} %reduce.9) | copy-start | bytes 3844
  5.2 1.6 %copy-start.15 = (pred[16,3]{0,1:T(4,128)(4,1)S(1)}, pred[16,3]{0,1:T(4,128)(4,1)}, u32[]{:S(2)}) copy-start(pred[16,3]{0,1:T(4,128)(4,1)} %constant.59) | copy-start | bytes 148
  9.3 1.4 %copy-start.11 = (f32[1,320]{1,0:T(1,128)S(1)}, f32[1,320]{1,0:T(1,128)}, u32[]{:S(2)}) copy-start(f32[1,320]{1,0:T(1,128)} %param.17) | copy-start | bytes 3844
  9.4 1.4 %copy-start.5 = (bf16[2,16,16,320]{3,2,1,0:T(8,128)(2,1)S(1)}, bf16[2,16,16,320]{3,2,1,0:T(8,128)(2,1)}, u32[]{:S(2)}) copy-start(bf16[2,16,16,320]{3,2,1,0:T(8,128)(2,1)} %param.12) | copy-start | bytes 983044
  12.8 8.6 %copy-start.6 = (bf16[2,16,16,320]{3,2,1,0:T(8,128)(2,1)S(1)}, bf16[2,16,16,320]{3,2,1,0:T(8,128)(2,1)}, u32[]{:S(2)}) copy-start(bf16[2,16,16,320]{3,2,1,0:T(8,128)(2,1)} %param.13) | copy-start | bytes 983044
  12.8 42.2 %collective-permute-start = (bf16[2,16,16,320]{3,1,2,0:T(8,128)(2,1)}, bf16[2,16,16,320]{3,1,2,0:T(8,128)(2,1)}, u32[]{:S(2)}, u32[]{:S(2)}) collective-permute-start(bf16[2,16,16,320]{3,1,2,0:T(8,128)(2,1)} %fusion.65), channel_id=1, source_target_pairs={{0,32},{32,64},{64,96},{96,128},{128,160},{160,192},{192,224},{224... | collective-permute-start | bytes 983048 | tf_op jit(solution)/shard_map/ppermute | solution.py:19
  14.7 43.1 %collective-permute-start.2 = (bf16[2,16,16,320]{3,1,2,0:T(8,128)(2,1)}, bf16[2,16,16,320]{3,1,2,0:T(8,128)(2,1)}, u32[]{:S(2)}, u32[]{:S(2)}) collective-permute-start(bf16[2,16,16,320]{3,1,2,0:T(8,128)(2,1)} %fusion.65), channel_id=1, source_target_pairs={{0,32},{32,0},{64,96},{96,64},{128,160},{160,128},{192,224},{224,1... | collective-permute-start | bytes 983048 | tf_op jit(solution)/shard_map/ppermute | solution.py:13
  25.1 3.6 %copy-start.2 = (bf16[2,16,16,16,20]{4,3,2,1,0:T(8,128)(2,1)S(1)}, bf16[2,16,16,16,20]{4,3,2,1,0:T(8,128)(2,1)}, u32[]{:S(2)}) copy-start(bf16[2,16,16,16,20]{4,3,2,1,0:T(8,128)(2,1)} %concatenate.27) | copy-start | bytes 983044
  25.1 3.6 %copy-start.4 = (bf16[2,16,16,16,20]{4,3,2,1,0:T(8,128)(2,1)S(1)}, bf16[2,16,16,16,20]{4,3,2,1,0:T(8,128)(2,1)}, u32[]{:S(2)}) copy-start(bf16[2,16,16,16,20]{4,3,2,1,0:T(8,128)(2,1)} %concatenate.26) | copy-start | bytes 983044
  35.4 7.7 %copy-start.10 = (f32[1,640]{1,0:T(1,128)S(1)}, f32[1,640]{1,0:T(1,128)}, u32[]{:S(2)}) copy-start(f32[1,640]{1,0:T(1,128)} %param.22) | copy-start | bytes 7684
  44.6 2.0 %copy-start.13 = (bf16[1,3,3,640,320]{3,4,2,1,0:T(8,128)(2,1)S(1)}, bf16[1,3,3,640,320]{3,4,2,1,0:T(8,128)(2,1)}, u32[]{:S(2)}) copy-start(bf16[1,3,3,640,320]{3,4,2,1,0:T(8,128)(2,1)} %param.20) | copy-start | bytes 11059204
  44.6 2.0 %copy-start.16 = (pred[16,3]{0,1:T(4,128)(4,1)S(1)}, pred[16,3]{0,1:T(4,128)(4,1)}, u32[]{:S(2)}) copy-start(pred[16,3]{0,1:T(4,128)(4,1)} %constant.59) | copy-start | bytes 148
  51.4 0.7 copy-start.12
  52.1 5.1 %copy-start.9 = (f32[320]{0:T(512)S(1)}, f32[320]{0:T(512)}, u32[]{:S(2)}) copy-start(f32[320]{0:T(512)} %copy-done.8) | copy-start | bytes 3844
  54.0 21.3 %collective-permute-start.1 = (bf16[2,16,16,320]{3,1,2,0:T(8,128)(2,1)}, bf16[2,16,16,320]{3,1,2,0:T(8,128)(2,1)}, u32[]{:S(2)}, u32[]{:S(2)}) collective-permute-start(bf16[2,16,16,320]{3,1,2,0:T(8,128)(2,1)} %fusion.73), channel_id=1, source_target_pairs={{0,32},{32,64},{64,96},{96,128},{128,160},{160,192},{192,224},{224... | collective-permute-start | bytes 983048 | tf_op jit(solution)/shard_map/ppermute | solution.py:19
  57.8 16.2 %collective-permute-start.3 = (bf16[2,16,16,320]{3,1,2,0:T(8,128)(2,1)}, bf16[2,16,16,320]{3,1,2,0:T(8,128)(2,1)}, u32[]{:S(2)}, u32[]{:S(2)}) collective-permute-start(bf16[2,16,16,320]{3,1,2,0:T(8,128)(2,1)} %collective-permute-done.2), channel_id=1, source_target_pairs={{0,64},{32,96},{64,0},{96,32},{128,192},{160,224},{192,128},{224,1... | collective-permute-start | bytes 983048 | tf_op jit(solution)/shard_map/ppermute | solution.py:13
  61.3 20.1 %collective-permute-start.5 = (bf16[2,16,16,320]{3,1,2,0:T(8,128)(2,1)S(1)}, bf16[2,16,16,320]{3,1,2,0:T(8,128)(2,1)}, u32[]{:S(2)}, u32[]{:S(2)}) collective-permute-start(bf16[2,16,16,320]{3,1,2,0:T(8,128)(2,1)S(1)} %fusion.67), channel_id=1, source_target_pairs={{0,32},{32,0},{64,96},{96,64},{128,160},{160,128},{192,224},{224,1... | collective-permute-start | bytes 983048 | tf_op jit(solution)/shard_map/ppermute | solution.py:13
  74.0 13.7 %collective-permute-start.4 = (bf16[2,16,16,320]{3,1,2,0:T(8,128)(2,1)}, bf16[2,16,16,320]{3,1,2,0:T(8,128)(2,1)S(1)}, u32[]{:S(2)}, u32[]{:S(2)}) collective-permute-start(bf16[2,16,16,320]{3,1,2,0:T(8,128)(2,1)} %collective-permute-done.3), channel_id=1, source_target_pairs={{0,128},{32,160},{64,192},{96,224},{128,0},{160,32},{192,64},{224,... | collective-permute-start | bytes 983048 | tf_op jit(solution)/shard_map/ppermute | solution.py:13
  79.1 8.5 %copy-start.7 = (bf16[2,16,16,320]{3,2,1,0:T(8,128)(2,1)S(1)}, bf16[2,16,16,320]{3,2,1,0:T(8,128)(2,1)}, u32[]{:S(2)}) copy-start(bf16[2,16,16,320]{3,2,1,0:T(8,128)(2,1)} %get-tuple-element.9) | copy-start | bytes 983044
  81.4 34.7 %collective-permute-start.6 = (bf16[2,16,16,320]{3,1,2,0:T(8,128)(2,1)}, bf16[2,16,16,320]{3,1,2,0:T(8,128)(2,1)}, u32[]{:S(2)}, u32[]{:S(2)}) collective-permute-start(bf16[2,16,16,320]{3,1,2,0:T(8,128)(2,1)} %collective-permute-done.5), channel_id=1, source_target_pairs={{0,64},{32,96},{64,0},{96,32},{128,192},{160,224},{192,128},{224,1... | collective-permute-start | bytes 983048 | tf_op jit(solution)/shard_map/ppermute | solution.py:13
  91.5 2.7 %copy-start.3 = (bf16[2,16,16,16,20]{4,3,1,2,0:T(8,128)(2,1)S(1)}, bf16[2,16,16,16,20]{4,3,1,2,0:T(8,128)(2,1)}, u32[]{:S(2)}) copy-start(bf16[2,16,16,16,20]{4,3,1,2,0:T(8,128)(2,1)} %concatenate.30) | copy-start | bytes 983044
  108.8 2.0 %copy-start.14 = (bf16[1,3,3,640,320]{3,4,2,1,0:T(8,128)(2,1)S(1)}, bf16[1,3,3,640,320]{3,4,2,1,0:T(8,128)(2,1)}, u32[]{:S(2)}) copy-start(bf16[1,3,3,640,320]{3,4,2,1,0:T(8,128)(2,1)} %param.20) | copy-start | bytes 11059204
  116.0 11.0 %collective-permute-start.7 = (bf16[2,16,16,320]{3,1,2,0:T(8,128)(2,1)}, bf16[2,16,16,320]{3,1,2,0:T(8,128)(2,1)S(1)}, u32[]{:S(2)}, u32[]{:S(2)}) collective-permute-start(bf16[2,16,16,320]{3,1,2,0:T(8,128)(2,1)} %collective-permute-done.6), channel_id=1, source_target_pairs={{0,128},{32,160},{64,192},{96,224},{128,0},{160,32},{192,64},{224,... | collective-permute-start | bytes 983048 | tf_op jit(solution)/shard_map/ppermute | solution.py:13
  117.6 10.6 %copy-start.1 = (bf16[1,3,3,320,320]{4,3,2,1,0:T(8,128)(2,1)S(1)}, bf16[1,3,3,320,320]{4,3,2,1,0:T(8,128)(2,1)}, u32[]{:S(2)}) copy-start(bf16[1,3,3,320,320]{4,3,2,1,0:T(8,128)(2,1)} %param.16) | copy-start | bytes 5529604
where the time goes:
time: 129 us; the launch traced here: 128 us
  local copies, waits for them, and re-layouts  43.6 us (34%)
  other arithmetic  35.6 us (28%)
  waiting for transfers between devices  23.7 us (18%)
  matrix products  14.6 us (11%)
  starting transfers between devices  9.63 us (7%)
    ppermute x6, waiting for transfers between devices, from_partner(): return lax.ppermute(value, axis, pairs)  23.7 us
    convert_element_type x2, local copies, waits for them, and re-layouts, decode(): joined = jnp.concatenate([current, skipped], axis=3).astype(jnp.float32)  15.5 us
    conv_general_dilated x4, matrix products, convolve(): lax.conv_general_dilated(inputs, kernel, (1, 1), 'SAME', dimension_number...  14.6 us
    concatenate x4, local copies, waits for them, and re-layouts, decode(): joined = jnp.concatenate([current, skipped], axis=3).astype(jnp.float32)  13.9 us
    reduce_sum x6, other arithmetic, norm_silu(): average = jnp.mean(grouped, axis=(1, 2, 4), keepdims=True)  9 us
    convert_element_type x2, other arithmetic, decode(): joined = jnp.concatenate([current, skipped], axis=3).astype(jnp.float32)  8.22 us
    unnamed x39, local copies, waits for them, and re-layouts  7.39 us
    ppermute x6, starting transfers between devices, from_partner(): return lax.ppermute(value, axis, pairs)  6.71 us
  transfers between devices with their start and end apart: 8, of which 3 were waited for; matrix products, arithmetic and copies ran while one was open for 60% of the time, Pallas kernels for 0%

commit v1 on v0

v1 whole, which is shorter than its diff:
```python
import jax
import jax.numpy as jnp
from jax import lax
from jax.experimental import pallas as pl
from jax.experimental.pallas import tpu as pltpu
from jax.sharding import PartitionSpec as P

GROUPS = 32
TICKS = 2
IMAGES = 2
SIDE = 16
CELLS = SIDE * SIDE
HALF = CELLS // 2
C = 320
ROWS = IMAGES * CELLS
TAPS = 3 * C
F32 = jnp.float32
BF16 = jnp.bfloat16
ANY = pl.BlockSpec(memory_space=pl.ANY)
VMEM = pl.BlockSpec(memory_space=pltpu.VMEM)
SMEM = pl.BlockSpec(memory_space=pltpu.SMEM)


def group_matrix(width):
    scale = 65536 // width + 1
    rows = lax.shift_right_logical(lax.broadcasted_iota(jnp.int32, (C, C), 0) * scale, 16)
    cols = lax.shift_right_logical(lax.broadcasted_iota(jnp.int32, (C, C), 1) * scale, 16)
    return jnp.where(rows == cols, 1.0, 0.0).astype(BF16)


def column_parts(values):
    return jnp.sum(values.reshape(CELLS // 8, 8, C), axis=0)


def group_means(parts, matrix, width):
    pieces = []
    for part in parts:
        high = part.astype(BF16).astype(F32)
        rest = part - high
        middle = rest.astype(BF16).astype(F32)
        pieces += [high, middle, rest - middle]
    stacked = jnp.concatenate(pieces, axis=0).astype(BF16)
    sums = jnp.dot(stacked, matrix, preferred_element_type=F32)
    weight = 1.0 / (width * CELLS)
    return [jnp.sum(sums[24 * i : 24 * (i + 1)], axis=0, keepdims=True) * weight for i in range(len(parts))]


def norm_all(loads, gains, betas, width):
    matrix = group_matrix(width)
    means = group_means([column_parts(load().astype(F32)) for load in loads], matrix, width)
    squares = []
    for load, mean in zip(loads, means):
        centred = load().astype(F32) - mean
        squares.append(column_parts(centred * centred))
    variances = group_means(squares, matrix, width)
    results = []
    for load, mean, variance, gain, beta in zip(loads, means, variances, gains, betas):
        half = ((load().astype(F32) - mean) * (lax.rsqrt(variance + 1e-05) * gain) + beta) * 0.5
        results.append((half * jnp.tanh(half) + half).astype(BF16))
    return results


def spread_rows(hidden):
    blank = jnp.zeros((SIDE, C), BF16)
    above = jnp.concatenate([blank, hidden[: CELLS - SIDE]], axis=0)
    below = jnp.concatenate([hidden[SIDE:], blank], axis=0)
    return jnp.concatenate([above, hidden, below], axis=1)


def gather_columns(sums):
    column = lax.broadcasted_iota(jnp.int32, (CELLS, C), 0) & (SIDE - 1)
    left = jnp.where(column > 0, pltpu.roll(sums[:, :C], 1, 0), 0.0)
    right = jnp.where(column < SIDE - 1, pltpu.roll(sums[:, 2 * C :], CELLS - 1, 0), 0.0)
    return left + sums[:, C : 2 * C] + right


def pack(value):
    return jnp.concatenate([value[:HALF], value[HALF:]], axis=1)


def unpack(value):
    return jnp.concatenate([value[:, :C], value[:, C:]], axis=0)


def copy_in(source, target, semaphore):
    copy = pltpu.make_async_copy(source, target, semaphore)
    copy.start()
    return copy


def make_enc(turn):
    def body(*refs):
        if turn == 0:
            source, weight, bias, gain, beta, out, send, *scratch = refs
        else:
            place, fresh, received, _, weight, bias, gain, beta, out, send, *scratch = refs
        current, kernel, taps, wide, sums, result, sems = scratch
        weight_copy = copy_in(weight, kernel, sems.at[0])
        if turn == 0:
            copy_in(source, current, sems.at[1]).wait()
        else:
            leading = place[0] == 0

            @pl.when(leading)
            def _():
                copy_in(fresh, current, sems.at[1]).wait()

            @pl.when(jnp.logical_not(leading))
            def _():
                for i in range(IMAGES):
                    current[pl.ds(i * CELLS, CELLS)] = unpack(received[i])

        loads = [lambda i=i: current[pl.ds(i * CELLS, CELLS)] for i in range(IMAGES)]
        hidden = norm_all(loads, [gain[...]] * IMAGES, [beta[...]] * IMAGES, C // GROUPS)
        for i in range(IMAGES):
            wide[pl.ds(i * CELLS, CELLS)] = spread_rows(hidden[i])
        weight_copy.wait()
        for ky in range(3):
            taps[pl.ds(ky * C, C)] = jnp.concatenate([kernel[ky, kx] for kx in range(3)], axis=1)
        sums[...] = jnp.dot(wide[...], taps[...], preferred_element_type=F32)
        copies = []
        for i in range(IMAGES):
            rows = pl.ds(i * CELLS, CELLS)
            total = (current[rows].astype(F32) + gather_columns(sums[rows]) + bias[...]).astype(BF16)
            result[rows] = total
            send[i] = pack(total)
            copies.append(copy_in(result.at[rows], out.at[pl.ds(turn * ROWS + i * CELLS, CELLS)], sems.at[2 + i]))
        for copy in copies:
            copy.wait()

    scratch = [
        pltpu.VMEM((ROWS, C), BF16),
        pltpu.VMEM((3, 3, C, C), BF16),
        pltpu.VMEM((TAPS, TAPS), BF16),
        pltpu.VMEM((ROWS, TAPS), BF16),
        pltpu.VMEM((ROWS, TAPS), F32),
        pltpu.VMEM((ROWS, C), BF16),
        pltpu.SemaphoreType.DMA((4,)),
    ]
    out_shape = (
        jax.ShapeDtypeStruct((TICKS * ROWS, C), BF16),
        jax.ShapeDtypeStruct((IMAGES, HALF, 2 * C), BF16),
    )
    if turn == 0:
        return pl.pallas_call(
            body,
            out_shape=out_shape,
            in_specs=[ANY, ANY, VMEM, VMEM, VMEM],
            out_specs=(ANY, VMEM),
            scratch_shapes=scratch,
            name="enc_first",
        )
    return pl.pallas_call(
        body,
        out_shape=out_shape,
        in_specs=[SMEM, ANY, VMEM, ANY, ANY, VMEM, VMEM, VMEM],
        out_specs=(ANY, VMEM),
        scratch_shapes=scratch,
        input_output_aliases={3: 0},
        name="enc_second",
    )


def make_dec(turn):
    def body(*refs):
        if turn == 0:
            source, skips, weight, bias, gain, beta, out, send, *scratch = refs
        else:
            place, received_enc, received_dec, skips, _, weight, bias, gain, beta, out, *scratch = refs
        current, skipped, kernel, taps, wide, sums, result, sems = scratch
        weight_copy = copy_in(weight, kernel, sems.at[0])
        if turn == 0:
            first = copy_in(source, current, sems.at[1])
            second = copy_in(skips.at[pl.ds(0, ROWS)], skipped, sems.at[2])
            first.wait()
            second.wait()
        else:
            leading = place[0] == 0

            @pl.when(leading)
            def _():
                for i in range(IMAGES):
                    rows = pl.ds(i * CELLS, CELLS)
                    value = unpack(received_enc[i])
                    skipped[rows] = value
                    current[rows] = value

            @pl.when(jnp.logical_not(leading))
            def _():
                second = copy_in(skips.at[pl.ds(ROWS, ROWS)], skipped, sems.at[2])
                for i in range(IMAGES):
                    current[pl.ds(i * CELLS, CELLS)] = unpack(received_dec[i])
                second.wait()

        maps = (current, skipped)
        loads = [lambda m=m, i=i: m[pl.ds(i * CELLS, CELLS)] for m in maps for i in range(IMAGES)]
        gains = [gain[:, :C]] * IMAGES + [gain[:, C:]] * IMAGES
        betas = [beta[:, :C]] * IMAGES + [beta[:, C:]] * IMAGES
        hidden = norm_all(loads, gains, betas, 2 * C // GROUPS)
        for i in range(IMAGES):
            rows = pl.ds(i * CELLS, CELLS)
            wide[rows, :TAPS] = spread_rows(hidden[i])
            wide[rows, TAPS:] = spread_rows(hidden[IMAGES + i])
        weight_copy.wait()
        taps[:, :TAPS] = jnp.concatenate([kernel[ky, :, :C] for ky in range(3)], axis=1)
        taps[:, TAPS:] = jnp.concatenate([kernel[ky, :, C:] for ky in range(3)], axis=1)
        sums[...] = lax.dot_general(wide[...], taps[...], (((1,), (1,)), ((), ())), preferred_element_type=F32)
        copies = []
        for i in range(IMAGES):
            rows = pl.ds(i * CELLS, CELLS)
            total = (current[rows].astype(F32) + gather_columns(sums[rows]) + bias[...]).astype(BF16)
            if turn == 0:
                send[i] = pack(total)
            result[rows] = total
            copies.append(copy_in(result.at[rows], out.at[pl.ds(turn * ROWS + i * CELLS, CELLS)], sems.at[3 + i]))
        for copy in copies:
            copy.wait()

    scratch = [
        pltpu.VMEM((ROWS, C), BF16),
        pltpu.VMEM((ROWS, C), BF16),
        pltpu.VMEM((3, TAPS, 2 * C), BF16),
        pltpu.VMEM((TAPS, 2 * TAPS), BF16),
        pltpu.VMEM((ROWS, 2 * TAPS), BF16),
        pltpu.VMEM((ROWS, TAPS), F32),
        pltpu.VMEM((ROWS, C), BF16),
        pltpu.SemaphoreType.DMA((5,)),
    ]
    whole = jax.ShapeDtypeStruct((TICKS * ROWS, C), BF16)
    if turn == 0:
        return pl.pallas_call(
            body,
            out_shape=(whole, jax.ShapeDtypeStruct((IMAGES, HALF, 2 * C), BF16)),
            in_specs=[ANY, ANY, ANY, VMEM, VMEM, VMEM],
            out_specs=(ANY, VMEM),
            scratch_shapes=scratch,
            name="dec_first",
        )
    return pl.pallas_call(
        body,
        out_shape=whole,
        in_specs=[SMEM, VMEM, VMEM, ANY, ANY, ANY, VMEM, VMEM, VMEM],
        out_specs=ANY,
        scratch_shapes=scratch,
        input_output_aliases={4: 0},
        name="dec_second",
    )


def make_queue(turn):
    def body(*refs):
        if turn == 0:
            place, direct, shifted, out, result, sems = refs
            shared = jnp.logical_or(place[0] == 0, place[0] == 4)
        else:
            direct, _, out, result, sems = refs
        copies = []
        for i in range(IMAGES):
            value = direct[i]
            if turn == 0:
                value = jnp.where(shared, shifted[i], value)
            rows = pl.ds(i * CELLS, CELLS)
            result[rows] = unpack(value)
            copies.append(copy_in(result.at[rows], out.at[pl.ds(turn * ROWS + i * CELLS, CELLS)], sems.at[i]))
        for copy in copies:
            copy.wait()

    return pl.pallas_call(
        body,
        out_shape=jax.ShapeDtypeStruct((TICKS * ROWS, C), BF16),
        in_specs=[SMEM, VMEM, VMEM] if turn == 0 else [VMEM, ANY],
        out_specs=ANY,
        scratch_shapes=[pltpu.VMEM((ROWS, C), BF16), pltpu.SemaphoreType.DMA((IMAGES,))],
        input_output_aliases={} if turn == 0 else {1: 0},
        name="queue_first" if turn == 0 else "queue_second",
    )


def shards(
    enc_in,
    dec_in,
    fresh,
    skip_queue,
    enc_weight,
    enc_bias,
    enc_gain,
    enc_beta,
    dec_weight,
    dec_bias,
    dec_gain,
    dec_beta,
):
    place = lax.axis_index("section").astype(jnp.int32).reshape(1)
    forward = [(s, (s + 1) % 8) for s in range(8)]
    mirror = [(s, 7 - s) for s in range(8)]
    enc_kernel = enc_weight.reshape(3, 3, C, C)
    dec_kernel = jnp.transpose(dec_weight, (0, 1, 2, 4, 3)).reshape(3, TAPS, 2 * C)
    skips = skip_queue.reshape(TICKS * ROWS, C)

    encoded, enc_sent = make_enc(0)(enc_in.reshape(ROWS, C), enc_kernel, enc_bias, enc_gain, enc_beta)
    enc_moved = lax.ppermute(enc_sent, "section", forward)
    decoded, dec_sent = make_dec(0)(dec_in.reshape(ROWS, C), skips, dec_kernel, dec_bias, dec_gain, dec_beta)
    dec_moved = lax.ppermute(dec_sent, "section", [pair for pair in forward if pair[1] != 0])
    enc_turned = lax.ppermute(enc_sent, "section", [pair for pair in mirror if pair[1] not in (0, 4)])
    encoded, last_sent = make_enc(1)(
        place, fresh.reshape(ROWS, C), enc_moved, encoded, enc_kernel, enc_bias, enc_gain, enc_beta
    )
    last_turned = lax.ppermute(last_sent, "section", mirror)
    decoded = make_dec(1)(
        place, enc_moved, dec_moved, skips, decoded, dec_kernel, dec_bias, dec_gain, dec_beta
    )
    queued = make_queue(0)(place, enc_turned, enc_moved)
    queued = make_queue(1)(last_turned, queued)
    shape = (TICKS * IMAGES, SIDE, SIDE, C)
    return encoded.reshape(shape), decoded.reshape(shape), queued.reshape(shape)


def solution(mesh):
    maps = P(("dp", "section"), None, None, None)
    rows = P("section", None)
    kernels = P("section", None, None, None, None)
    in_specs = (maps, maps, P("dp", None, None, None), maps) + (kernels, rows, rows, rows) * 2
    return jax.shard_map(shards, mesh=mesh, in_specs=in_specs, out_specs=(maps, maps, maps), check_vma=False)
```

time: 129 us -> 47.4 us (0.37)
  the two profiles are of different devices: /device:TPU:82 before, /device:TPU:46 now
where the time goes in v1:
time: 47.4 us; the launch traced here: 47 us
  Pallas kernels  32.2 us (68%)
  starting transfers between devices  11 us (23%)
  local copies, waits for them, and re-layouts  2.9 us (6%)
  between operations  0.9 us (2%)
    pallas_call x1, Pallas kernels, shards(): make_dec(0)  8.62 us
    ppermute x1, starting transfers between devices, shards(): last_turned = lax.ppermute(last_sent, 'section', mirror)  8.34 us
    pallas_call x1, Pallas kernels, shards(): make_dec(1)  8.13 us
    pallas_call x1, Pallas kernels, shards(): make_enc(0)  6.14 us
    pallas_call x1, Pallas kernels, shards(): make_enc(1)  5.55 us
    unnamed x8, local copies, waits for them, and re-layouts  2.9 us
    pallas_call x1, Pallas kernels, shards(): queued = make_queue(0)(place, enc_turned, enc_moved)  1.93 us
    pallas_call x1, Pallas kernels, shards(): queued = make_queue(1)(last_turned, queued)  1.82 us
  transfers between devices with their start and end apart: 4, of which 0 were waited for; matrix products, arithmetic and copies ran while one was open for 0% of the time, Pallas kernels for 52%

profile of v1, /device:TPU:46, one launch (start us, length us, event | category | flops | bytes accessed | tf_op | source)
XLA Modules:
  0.0 47.0 jit_solution(12824965367138718690)
XLA Ops:
  0.6 6.1 %enc_first.1 = (bf16[1024,320]{1,0:T(8,128)(2,1)}, bf16[2,128,640]{2,1,0:T(8,128)(2,1)}) custom-call(bf16[512,320]{1,0:T(8,128)(2,1)} %bitcast.22, bf16[3,3,320,320]{3,2,1,0:T(8,128)(2,1)} %bitcast.14, f32[1,320]{1,0:T(1,128)} %refs_5_.2, f32[1,320]{1,0:T(1,128)} %refs_6_.2, f32[1,320]{1,0:T(1,128)} %refs_7_.2), custom_call_target="tpu_custom_call" | custom-call | tf_op jit(solution)/shard_map/enc_first/pallas_call | solution.py:300
  6.8 0.1 collective-permute-start
  6.9 1.3 %collective-permute-start.3 = (bf16[2,128,640]{2,1,0:T(8,128)(2,1)}, bf16[2,128,640]{2,1,0:T(8,128)(2,1)S(1)}, u32[]{:S(2)}, u32[]{:S(2)}) collective-permute-start(bf16[2,128,640]{2,1,0:T(8,128)(2,1)} %get-tuple-element.9), channel_id=1, source_target_pairs={{0,224},{32,192},{64,160},{128,96},{160,64},{192,32},{1,225},{33,1... | collective-permute-start | bytes 983048 | tf_op jit(solution)/shard_map/ppermute | solution.py:304
  8.2 8.6 %dec_first.1 = (bf16[1024,320]{1,0:T(8,128)(2,1)}, bf16[2,128,640]{2,1,0:T(8,128)(2,1)}) custom-call(bf16[512,320]{1,0:T(8,128)(2,1)} %bitcast.23, bf16[1024,320]{1,0:T(8,128)(2,1)} %bitcast.16, bf16[3,960,640]{2,1,0:T(8,128)(2,1)} %bitcast.12, f32[1,320]{1,0:T(1,128)} %refs_6_.3, f32[1,640]{1,0:T(1,128)} %refs_7_.3, f32[1,640]{1,0:T(1,128)} %refs_8_.1), custom_call_target="tpu_custom_call" | custom-call | tf_op jit(solution)/shard_map/dec_first/pallas_call | solution.py:302
  16.8 1.3 %collective-permute-start.1 = (bf16[2,128,640]{2,1,0:T(8,128)(2,1)}, bf16[2,128,640]{2,1,0:T(8,128)(2,1)S(1)}, u32[]{:S(2)}, u32[]{:S(2)}) collective-permute-start(bf16[2,128,640]{2,1,0:T(8,128)(2,1)} %get-tuple-element.12), channel_id=1, source_target_pairs={{0,32},{32,64},{64,96},{96,128},{128,160},{160,192},{192,224},{1,3... | collective-permute-start | bytes 983048 | tf_op jit(solution)/shard_map/ppermute | solution.py:303
  18.1 0.0 collective-permute-done.refs_2_.refs_1_
  18.1 0.0 copy-start
  18.1 0.7 %copy-done = bf16[2,128,640]{2,1,0:T(8,128)(2,1)} copy-done((bf16[2,128,640]{2,1,0:T(8,128)(2,1)}, bf16[2,128,640]{2,1,0:T(8,128)(2,1)S(1)}, u32[]{:S(2)}) %copy-start) | copy-done | bytes 327704
  18.8 5.6 %enc_second.1 = (bf16[1024,320]{1,0:T(8,128)(2,1)}, bf16[2,128,640]{2,1,0:T(8,128)(2,1)}) custom-call(s32[1]{0:T(128)} %bitcast.refs_0_, bf16[512,320]{1,0:T(8,128)(2,1)} %bitcast.21, bf16[2,128,640]{2,1,0:T(8,128)(2,1)} %copy-done, bf16[1024,320]{1,0:T(8,128)(2,1)} %get-tuple-element.10.refs_3_, ...), custom_call_target="tpu_custom_call", output_to_operand_aliasing={{0}: (3, {})} | custom-call | tf_op jit(solution)/shard_map/enc_second/pallas_call | solution.py:305
  24.4 8.3 %collective-permute-start.2 = (bf16[2,128,640]{2,1,0:T(8,128)(2,1)}, bf16[2,128,640]{2,1,0:T(8,128)(2,1)S(1)}, u32[]{:S(2)}, u32[]{:S(2)}) collective-permute-start(bf16[2,128,640]{2,1,0:T(8,128)(2,1)} %get-tuple-element.14), channel_id=1, source_target_pairs={{0,224},{32,192},{64,160},{96,128},{128,96},{160,64},{192,32},{224... | collective-permute-start | bytes 983048 | tf_op jit(solution)/shard_map/ppermute | solution.py:308
  32.7 0.0 collective-permute-done.3.refs_1_
  32.7 0.0 copy-start.2
  32.8 0.7 %copy-done.2 = bf16[2,128,640]{2,1,0:T(8,128)(2,1)} copy-done((bf16[2,128,640]{2,1,0:T(8,128)(2,1)}, bf16[2,128,640]{2,1,0:T(8,128)(2,1)S(1)}, u32[]{:S(2)}) %copy-start.2) | copy-done | bytes 327704
  33.5 1.9 %queue_first.1.refs_1_ = bf16[1024,320]{1,0:T(8,128)(2,1)} custom-call(s32[1]{0:T(128)} %bitcast.refs_0_, bf16[2,128,640]{2,1,0:T(8,128)(2,1)} %copy-done.2, bf16[2,128,640]{2,1,0:T(8,128)(2,1)} %copy-done), custom_call_target="tpu_custom_call" | custom-call | tf_op jit(solution)/shard_map/queue_first/pallas_call | solution.py:312
  35.4 0.0 collective-permute-done.1.refs_2_
  35.4 0.0 copy-start.1
  35.4 0.7 %copy-done.1 = bf16[2,128,640]{2,1,0:T(8,128)(2,1)} copy-done((bf16[2,128,640]{2,1,0:T(8,128)(2,1)}, bf16[2,128,640]{2,1,0:T(8,128)(2,1)S(1)}, u32[]{:S(2)}) %copy-start.1) | copy-done | bytes 327704
  36.2 8.1 %dec_second.1 = bf16[1024,320]{1,0:T(8,128)(2,1)} custom-call(s32[1]{0:T(128)} %bitcast.refs_0_, bf16[2,128,640]{2,1,0:T(8,128)(2,1)} %copy-done, bf16[2,128,640]{2,1,0:T(8,128)(2,1)} %copy-done.1, bf16[1024,320]{1,0:T(8,128)(2,1)} %bitcast.17, bf16[1024,320]{1,0:T(8,128)(2,1)} %get-tuple-element.13.refs_4_, ...), custom_call_target="tpu_custom_call", output_to_operand_aliasing={{}: (4, {})} | custom-call | tf_op jit(solution)/shard_map/dec_second/pallas_call | solution.py:309
  44.3 0.0 collective-permute-done.2.refs_0_
  44.3 0.0 copy-start.3
  44.3 0.7 %copy-done.3 = bf16[2,128,640]{2,1,0:T(8,128)(2,1)} copy-done((bf16[2,128,640]{2,1,0:T(8,128)(2,1)}, bf16[2,128,640]{2,1,0:T(8,128)(2,1)S(1)}, u32[]{:S(2)}) %copy-start.3) | copy-done | bytes 327704
  45.0 1.8 %queue_second.1 = bf16[1024,320]{1,0:T(8,128)(2,1)} custom-call(bf16[2,128,640]{2,1,0:T(8,128)(2,1)} %copy-done.3, bf16[1024,320]{1,0:T(8,128)(2,1)} %queue_first.1.refs_1_), custom_call_target="tpu_custom_call", output_to_operand_aliasing={{}: (1, {})} | custom-call | tf_op jit(solution)/shard_map/queue_second/pallas_call | solution.py:313
Async XLA Ops:
  6.8 11.3 %collective-permute-start = (bf16[2,128,640]{2,1,0:T(8,128)(2,1)}, bf16[2,128,640]{2,1,0:T(8,128)(2,1)S(1)}, u32[]{:S(2)}, u32[]{:S(2)}) collective-permute-start(bf16[2,128,640]{2,1,0:T(8,128)(2,1)} %get-tuple-element.9), channel_id=1, source_target_pairs={{0,32},{32,64},{64,96},{96,128},{128,160},{160,192},{192,224},{224... | collective-permute-start | bytes 983048 | tf_op jit(solution)/shard_map/ppermute | solution.py:301
  6.9 25.9 %collective-permute-start.3 = (bf16[2,128,640]{2,1,0:T(8,128)(2,1)}, bf16[2,128,640]{2,1,0:T(8,128)(2,1)S(1)}, u32[]{:S(2)}, u32[]{:S(2)}) collective-permute-start(bf16[2,128,640]{2,1,0:T(8,128)(2,1)} %get-tuple-element.9), channel_id=1, source_target_pairs={{0,224},{32,192},{64,160},{128,96},{160,64},{192,32},{1,225},{33,1... | collective-permute-start | bytes 983048 | tf_op jit(solution)/shard_map/ppermute | solution.py:304
  16.8 18.6 %collective-permute-start.1 = (bf16[2,128,640]{2,1,0:T(8,128)(2,1)}, bf16[2,128,640]{2,1,0:T(8,128)(2,1)S(1)}, u32[]{:S(2)}, u32[]{:S(2)}) collective-permute-start(bf16[2,128,640]{2,1,0:T(8,128)(2,1)} %get-tuple-element.12), channel_id=1, source_target_pairs={{0,32},{32,64},{64,96},{96,128},{128,160},{160,192},{192,224},{1,3... | collective-permute-start | bytes 983048 | tf_op jit(solution)/shard_map/ppermute | solution.py:303
  18.1 0.7 %copy-start = (bf16[2,128,640]{2,1,0:T(8,128)(2,1)}, bf16[2,128,640]{2,1,0:T(8,128)(2,1)S(1)}, u32[]{:S(2)}) copy-start(bf16[2,128,640]{2,1,0:T(8,128)(2,1)S(1)} %collective-permute-done.refs_2_.refs_1_) | copy-start | bytes 983044
  24.4 19.9 %collective-permute-start.2 = (bf16[2,128,640]{2,1,0:T(8,128)(2,1)}, bf16[2,128,640]{2,1,0:T(8,128)(2,1)S(1)}, u32[]{:S(2)}, u32[]{:S(2)}) collective-permute-start(bf16[2,128,640]{2,1,0:T(8,128)(2,1)} %get-tuple-element.14), channel_id=1, source_target_pairs={{0,224},{32,192},{64,160},{96,128},{128,96},{160,64},{192,32},{224... | collective-permute-start | bytes 983048 | tf_op jit(solution)/shard_map/ppermute | solution.py:308
  32.7 0.7 %copy-start.2 = (bf16[2,128,640]{2,1,0:T(8,128)(2,1)}, bf16[2,128,640]{2,1,0:T(8,128)(2,1)S(1)}, u32[]{:S(2)}) copy-start(bf16[2,128,640]{2,1,0:T(8,128)(2,1)S(1)} %collective-permute-done.3.refs_1_) | copy-start | bytes 983044
  35.4 0.7 %copy-start.1 = (bf16[2,128,640]{2,1,0:T(8,128)(2,1)}, bf16[2,128,640]{2,1,0:T(8,128)(2,1)S(1)}, u32[]{:S(2)}) copy-start(bf16[2,128,640]{2,1,0:T(8,128)(2,1)S(1)} %collective-permute-done.1.refs_2_) | copy-start | bytes 983044
  44.3 0.7 %copy-start.3 = (bf16[2,128,640]{2,1,0:T(8,128)(2,1)}, bf16[2,128,640]{2,1,0:T(8,128)(2,1)S(1)}, u32[]{:S(2)}) copy-start(bf16[2,128,640]{2,1,0:T(8,128)(2,1)S(1)} %collective-permute-done.2.refs_0_) | copy-start | bytes 983044

commit v2 on v1

v2 whole, which is shorter than its diff:
```python
import jax
import jax.numpy as jnp
from jax import lax
from jax.experimental import pallas as pl
from jax.experimental.pallas import tpu as pltpu
from jax.sharding import PartitionSpec as P


GROUPS = 32
TICKS = 2
IMAGES = 2
SIDE = 16
CELLS = SIDE * SIDE
HALF = CELLS // 2
C = 320
ROWS = IMAGES * CELLS
TAPS = 3 * C
F32 = jnp.float32
BF16 = jnp.bfloat16
PARCEL = (IMAGES, HALF, 2 * C)
HBM = pl.BlockSpec(memory_space=pltpu.HBM)
VMEM = pl.BlockSpec(memory_space=pltpu.VMEM)
WHOLE = jax.ShapeDtypeStruct((TICKS * ROWS, C), BF16)


def group_matrix(width):
    scale = 65536 // width + 1
    rows = lax.shift_right_logical(lax.broadcasted_iota(jnp.int32, (C, C), 0) * scale, 16)
    cols = lax.shift_right_logical(lax.broadcasted_iota(jnp.int32, (C, C), 1) * scale, 16)
    return jnp.where(rows == cols, 1.0, 0.0).astype(BF16)


def column_parts(values):
    return jnp.sum(values.reshape(CELLS // 8, 8, C), axis=0)


def group_means(parts, matrix, width):
    pieces = []
    for part in parts:
        high = part.astype(BF16).astype(F32)
        rest = part - high
        middle = rest.astype(BF16).astype(F32)
        pieces += [high, middle, rest - middle]
    stacked = jnp.concatenate(pieces, axis=0).astype(BF16)
    sums = jnp.dot(stacked, matrix, preferred_element_type=F32)
    weight = 1.0 / (width * CELLS)
    return [jnp.sum(sums[24 * i : 24 * (i + 1)], axis=0, keepdims=True) * weight for i in range(len(parts))]


def norm_all(loads, gains, betas, width):
    matrix = group_matrix(width)
    means = group_means([column_parts(load().astype(F32)) for load in loads], matrix, width)
    squares = []
    for load, mean in zip(loads, means):
        centred = load().astype(F32) - mean
        squares.append(column_parts(centred * centred))
    variances = group_means(squares, matrix, width)
    results = []
    for load, mean, variance, gain, beta in zip(loads, means, variances, gains, betas):
        half = ((load().astype(F32) - mean) * (lax.rsqrt(variance + 1e-05) * gain) + beta) * 0.5
        results.append((half * jnp.tanh(half) + half).astype(BF16))
    return results


def spread_rows(hidden):
    blank = jnp.zeros((SIDE, C), BF16)
    above = jnp.concatenate([blank, hidden[: CELLS - SIDE]], axis=0)
    below = jnp.concatenate([hidden[SIDE:], blank], axis=0)
    return jnp.concatenate([above, hidden, below], axis=1)


def gather_columns(sums):
    column = lax.broadcasted_iota(jnp.int32, (CELLS, C), 0) & (SIDE - 1)
    left = jnp.where(column > 0, pltpu.roll(sums[:, :C], 1, 0), 0.0)
    right = jnp.where(column < SIDE - 1, pltpu.roll(sums[:, 2 * C :], CELLS - 1, 0), 0.0)
    return left + sums[:, C : 2 * C] + right


def pack(value):
    return jnp.concatenate([value[:HALF], value[HALF:]], axis=1)


def unpack(value):
    return jnp.concatenate([value[:, :C], value[:, C:]], axis=0)


def begin(source, target, semaphore):
    copy = pltpu.make_async_copy(source, target, semaphore)
    copy.start()
    return copy


def image(index, base=0):
    return pl.ds(base + index * CELLS, CELLS)


def placed(value, spec):
    return pltpu.with_memory_space_constraint(value, pltpu.VMEM if spec is VMEM else pltpu.HBM)


def call(body, inputs, in_specs, outputs, scratch=(), aliases=None):
    held = [placed(value, spec) for value, spec in zip(inputs, in_specs)]
    return pl.pallas_call(
        body,
        out_shape=tuple(outputs),
        in_specs=list(in_specs),
        out_specs=tuple(HBM if isinstance(out, jax.ShapeDtypeStruct) else VMEM for out in outputs),
        scratch_shapes=list(scratch),
        input_output_aliases=aliases or {},
        compiler_params=pltpu.CompilerParams(vmem_limit_bytes=16 * 2**20),
    )(*held)


def enc_rest(current, gain, beta, bias, taps, wide, sums, send, ready=None):
    loads = [lambda i=i: current[image(i)] for i in range(IMAGES)]
    hidden = norm_all(loads, [gain[...]] * IMAGES, [beta[...]] * IMAGES, C // GROUPS)
    for i in range(IMAGES):
        wide[image(i)] = spread_rows(hidden[i])
    if ready is not None:
        ready()
    sums[...] = jnp.dot(wide[...], taps[...], preferred_element_type=F32)
    for i in range(IMAGES):
        total = current[image(i)].astype(F32) + gather_columns(sums[image(i)]) + bias[...]
        send[i] = pack(total.astype(BF16))


def enc_first(source, weight, enc_rows, later):
    count = len(later)

    def body(*refs):
        source, weight, bias, gain, beta = refs[:5]
        far = refs[5 : 5 + count]
        send, taps, bias_near, gain_near, beta_near = refs[5 + count : 10 + count]
        close = refs[10 + count : 10 + 2 * count]
        current, kernel, wide, sums, sems, later_sems = refs[10 + 2 * count :]
        first = [begin(source, current, sems.at[0])]
        first.append(begin(gain, gain_near, sems.at[1]))
        first.append(begin(beta, beta_near, sems.at[2]))
        first.append(begin(bias, bias_near, sems.at[3]))
        weights = [begin(weight.at[ky], kernel.at[ky], sems.at[4 + ky]) for ky in range(3)]
        fetched = [begin(far[k], close[k], later_sems.at[k]) for k in range(count)]
        for copy in first:
            copy.wait()

        def ready():
            for ky in range(3):
                weights[ky].wait()
                taps[pl.ds(ky * C, C)] = jnp.concatenate([kernel[ky, kx] for kx in range(3)], axis=1)

        enc_rest(current, gain_near, beta_near, bias_near, taps, wide, sums, send, ready)
        for copy in fetched:
            copy.wait()

    return call(
        body,
        (source, weight) + tuple(enc_rows) + tuple(later),
        [HBM] * (5 + count),
        [pltpu.VMEM(PARCEL, BF16), pltpu.VMEM((TAPS, TAPS), BF16)]
        + [pltpu.VMEM(row.shape, F32) for row in enc_rows]
        + [pltpu.VMEM(value.shape, value.dtype) for value in later],
        [
            pltpu.VMEM((ROWS, C), BF16),
            pltpu.VMEM((3, 3, C, C), BF16),
            pltpu.VMEM((ROWS, TAPS), BF16),
            pltpu.VMEM((ROWS, TAPS), F32),
            pltpu.SemaphoreType.DMA((7,)),
            pltpu.SemaphoreType.DMA((count,)),
        ],
    )


def write_maps(value, result, out, semaphores, base, slot):
    copies = []
    for i in range(IMAGES):
        result[image(i, slot * ROWS)] = unpack(value[i])
        copies.append(
            begin(result.at[image(i, slot * ROWS)], out.at[image(i, base)], semaphores.at[slot * IMAGES + i])
        )
    return copies


def enc_second(fresh, moved, taps, enc_rows, dec_sent):
    def body(fresh, moved, taps, bias, gain, beta, early, send, decoded, current, wide, sums, result, sems):
        copies = write_maps(early, result, decoded, sems, 0, 0)
        leading = lax.axis_index("section") == 0
        for i in range(IMAGES):
            current[image(i)] = jnp.where(leading, fresh[image(i)], unpack(moved[i]))
        enc_rest(current, gain, beta, bias, taps, wide, sums, send)
        for copy in copies:
            copy.wait()

    return call(
        body,
        (fresh, moved, taps) + tuple(enc_rows) + (dec_sent,),
        [VMEM] * 7,
        [pltpu.VMEM(PARCEL, BF16), WHOLE],
        [
            pltpu.VMEM((ROWS, C), BF16),
            pltpu.VMEM((ROWS, TAPS), BF16),
            pltpu.VMEM((ROWS, TAPS), F32),
            pltpu.VMEM((ROWS, C), BF16),
            pltpu.SemaphoreType.DMA((IMAGES,)),
        ],
    )


def multiply(wide, taps):
    return lax.dot_general(wide[...], taps[...], (((1,), (1,)), ((), ())), preferred_element_type=F32)


def dec_first(current, skips, kernel, dec_rows, enc_sent):
    def body(current, skips, kernel, bias, gain, beta, early, send, near, far, encoded, *scratch):
        wide, sums, result, sems = scratch
        taps = (near, far)
        copies = write_maps(early, result, encoded, sems, 0, 0)
        loads = [lambda m=m, i=i: m[image(i)] for m in (current, skips) for i in range(IMAGES)]
        gains = [gain[:, :C]] * IMAGES + [gain[:, C:]] * IMAGES
        betas = [beta[:, :C]] * IMAGES + [beta[:, C:]] * IMAGES
        hidden = norm_all(loads, gains, betas, 2 * C // GROUPS)
        for part in range(2):
            for i in range(IMAGES):
                wide[part, image(i)] = spread_rows(hidden[part * IMAGES + i])
            cut = slice(part * C, (part + 1) * C)
            taps[part][...] = jnp.concatenate([kernel[ky, :, cut] for ky in range(3)], axis=1)
        sums[...] = multiply(wide.at[0], near) + multiply(wide.at[1], far)
        for i in range(IMAGES):
            total = current[image(i)].astype(F32) + gather_columns(sums[image(i)]) + bias[...]
            send[i] = pack(total.astype(BF16))
        for copy in copies:
            copy.wait()

    return call(
        body,
        (current, skips, kernel) + tuple(dec_rows) + (enc_sent,),
        [VMEM] * 7,
        [pltpu.VMEM(PARCEL, BF16), pltpu.VMEM((TAPS, TAPS), BF16), pltpu.VMEM((TAPS, TAPS), BF16), WHOLE],
        [
            pltpu.VMEM((2, ROWS, TAPS), BF16),
            pltpu.VMEM((ROWS, TAPS), F32),
            pltpu.VMEM((ROWS, C), BF16),
            pltpu.SemaphoreType.DMA((IMAGES,)),
        ],
    )


def dec_skip(moved_enc, skips, taps, dec_rows, last_sent, encoded):
    def body(moved, skips, taps, bias, gain, beta, late, _, part, encoded, *scratch):
        result, skipped, wide, sums, sems = scratch
        copies = write_maps(late, result, encoded, sems, ROWS, 0)
        leading = lax.axis_index("section") == 0
        for i in range(IMAGES):
            skipped[image(i)] = jnp.where(leading, unpack(moved[i]), skips[image(i, ROWS)])
        loads = [lambda i=i: skipped[image(i)] for i in range(IMAGES)]
        hidden = norm_all(loads, [gain[:, C:]] * IMAGES, [beta[:, C:]] * IMAGES, 2 * C // GROUPS)
        for i in range(IMAGES):
            wide[image(i)] = spread_rows(hidden[i])
        sums[...] = multiply(wide, taps)
        for i in range(IMAGES):
            part[image(i)] = gather_columns(sums[image(i)]) + bias[...]
        for copy in copies:
            copy.wait()

    return call(
        body,
        (moved_enc, skips, taps) + tuple(dec_rows) + (last_sent, encoded),
        [VMEM] * 7 + [HBM],
        [pltpu.VMEM((ROWS, C), F32), WHOLE],
        [
            pltpu.VMEM((ROWS, C), BF16),
            pltpu.VMEM((ROWS, C), BF16),
            pltpu.VMEM((ROWS, TAPS), BF16),
            pltpu.VMEM((ROWS, TAPS), F32),
            pltpu.SemaphoreType.DMA((IMAGES,)),
        ],
        {7: 1},
    )


def dec_second(moved_enc, moved_dec, taps, part, dec_rows, decoded):
    def body(moved_enc, moved_dec, taps, part, gain, beta, _, out, *scratch):
        current, wide, sums, result, sems = scratch
        leading = lax.axis_index("section") == 0
        for i in range(IMAGES):
            current[image(i)] = unpack(jnp.where(leading, moved_enc[i], moved_dec[i]))
        loads = [lambda i=i: current[image(i)] for i in range(IMAGES)]
        hidden = norm_all(loads, [gain[:, :C]] * IMAGES, [beta[:, :C]] * IMAGES, 2 * C // GROUPS)
        for i in range(IMAGES):
            wide[image(i)] = spread_rows(hidden[i])
        sums[...] = multiply(wide, taps)
        copies = []
        for i in range(IMAGES):
            total = current[image(i)].astype(F32) + gather_columns(sums[image(i)]) + part[image(i)]
            result[image(i)] = total.astype(BF16)
            copies.append(begin(result.at[image(i)], out.at[image(i, ROWS)], sems.at[i]))
        for copy in copies:
            copy.wait()

    return call(
        body,
        (moved_enc, moved_dec, taps, part, dec_rows[1], dec_rows[2], decoded),
        [VMEM] * 6 + [HBM],
        [WHOLE],
        [
            pltpu.VMEM((ROWS, C), BF16),
            pltpu.VMEM((ROWS, TAPS), BF16),
            pltpu.VMEM((ROWS, TAPS), F32),
            pltpu.VMEM((ROWS, C), BF16),
            pltpu.SemaphoreType.DMA((IMAGES,)),
        ],
        {6: 0},
    )[0]


def queue_maps(turned, moved, last):
    def body(turned, moved, last, out, chosen, result, sems):
        shared = lax.axis_index("section") % 4 == 0
        for i in range(IMAGES):
            chosen[i] = jnp.where(shared, moved[i], turned[i])
        copies = write_maps(chosen, result, out, sems, 0, 0)
        copies += write_maps(last, result, out, sems, ROWS, 1)
        for copy in copies:
            copy.wait()

    return call(
        body,
        (turned, moved, last),
        [VMEM, VMEM, VMEM],
        [WHOLE],
        [
            pltpu.VMEM(PARCEL, BF16),
            pltpu.VMEM((2 * ROWS, C), BF16),
            pltpu.SemaphoreType.DMA((2 * IMAGES,)),
        ],
    )[0]


def shards(
    enc_in,
    dec_in,
    fresh,
    skip_queue,
    enc_weight,
    enc_bias,
    enc_gain,
    enc_beta,
    dec_weight,
    dec_bias,
    dec_gain,
    dec_beta,
):
    forward = [(s, (s + 1) % 8) for s in range(8)]
    mirror = [(s, 7 - s) for s in range(8)]
    relay = [(s, 8 - s) for s in range(1, 8) if s != 4]
    enc_kernel = enc_weight.reshape(3, 3, C, C)
    dec_kernel = jnp.transpose(dec_weight, (0, 1, 2, 4, 3)).reshape(3, TAPS, 2 * C)
    later = (
        dec_in.reshape(ROWS, C),
        skip_queue.reshape(TICKS * ROWS, C),
        dec_kernel,
        dec_bias,
        dec_gain,
        dec_beta,
        fresh.reshape(ROWS, C),
    )
    enc_sent, enc_taps, *held = enc_first(
        enc_in.reshape(ROWS, C), enc_kernel, (enc_bias, enc_gain, enc_beta), later
    )
    enc_rows, (dec_now, skips, dec_kernel), dec_rows, fresh_now = held[:3], held[3:6], held[6:9], held[9]
    moved_enc = lax.ppermute(enc_sent, "section", forward)
    dec_sent, dec_taps, skip_taps, encoded = dec_first(dec_now, skips, dec_kernel, dec_rows, enc_sent)
    moved_dec = lax.ppermute(dec_sent, "section", [pair for pair in forward if pair[1] != 0])
    turned = lax.ppermute(moved_enc, "section", relay)
    last_sent, decoded = enc_second(fresh_now, moved_enc, enc_taps, enc_rows, dec_sent)
    last = lax.ppermute(last_sent, "section", mirror)
    part, encoded = dec_skip(moved_enc, skips, skip_taps, dec_rows, last_sent, encoded)
    decoded = dec_second(moved_enc, moved_dec, dec_taps, part, dec_rows, decoded)
    queued = queue_maps(turned, moved_enc, last)
    shape = (TICKS * IMAGES, SIDE, SIDE, C)
    return encoded.reshape(shape), decoded.reshape(shape), queued.reshape(shape)


def solution(mesh):
    maps = P(("dp", "section"), None, None, None)
    rows = P("section", None)
    kernels = P("section", None, None, None, None)
    in_specs = (maps, maps, P("dp", None, None, None), maps) + (kernels, rows, rows, rows) * 2

    return jax.shard_map(shards, mesh=mesh, in_specs=in_specs, out_specs=(maps, maps, maps), check_vma=False)
```

time: 47.4 us -> 40 us (0.84)
  the two profiles are of different devices: /device:TPU:46 before, /device:TPU:82 now
where the time goes in v2:
time: 40 us; the launch traced here: 39.4 us
  Pallas kernels  18.1 us (45%)
  starting transfers between devices  10.6 us (26%)
  waiting for transfers between devices  9.88 us (25%)
  between operations  0.86 us (2%)
    pallas_call x6, Pallas kernels, call(): pl.pallas_call(body, out_shape=tuple(outputs), in_specs=list(in_specs), o...  18.1 us
    ppermute x1, waiting for transfers between devices, shards(): last = lax.ppermute(last_sent, 'section', mirror)  7.27 us
    ppermute x1, starting transfers between devices, shards(): lax.ppermute(dec_sent, 'section', [pair for pair in forward if pair[1] !=...  2.95 us
    ppermute x1, starting transfers between devices, shards(): turned = lax.ppermute(moved_enc, 'section', relay)  2.89 us
    ppermute x1, starting transfers between devices, shards(): last = lax.ppermute(last_sent, 'section', mirror)  2.74 us
    ppermute x1, starting transfers between devices, shards(): moved_enc = lax.ppermute(enc_sent, 'section', forward)  1.99 us
    ppermute x1, waiting for transfers between devices, shards(): moved_enc = lax.ppermute(enc_sent, 'section', forward)  1.5 us
    ppermute x1, waiting for transfers between devices, shards(): turned = lax.ppermute(moved_enc, 'section', relay)  1.1 us
  transfers between devices with their start and end apart: 4, of which 3 were waited for; matrix products, arithmetic and copies ran while one was open for 0% of the time, Pallas kernels for 30%

profile of v2, /device:TPU:82, one launch (start us, length us, event | category | flops | bytes accessed | tf_op | source)
XLA Modules:
  0.0 39.4 jit_solution(1477674460373438622)
XLA Ops:
  0.6 5.1 %shard_map.139 = (bf16[2,128,640]{2,1,0:T(8,128)(2,1)S(1)}, bf16[960,960]{1,0:T(8,128)(2,1)S(1)}, f32[1,320]{1,0:T(1,128)S(1)}, f32[1,320]{1,0:T(1,128)S(1)}, f3...) custom-call(bf16[512,320]{1,0:T(8,128)(2,1)} %bitcast.17, ...), custom_call_target="tpu_custom_call" | custom-call | tf_op jit(solution)/shard_map/pallas_call | solution.py:103
  5.8 2.0 %collective-permute-start = (bf16[2,128,640]{2,1,0:T(8,128)(2,1)S(1)}, bf16[2,128,640]{2,1,0:T(8,128)(2,1)S(1)}, u32[]{:S(2)}, u32[]{:S(2)}) collective-permute-start(bf16[2,128,640]{2,1,0:T(8,128)(2,1)S(1)} %get-tuple-element.23.early), channel_id=1, source_target_pairs={{0,32},{32,64},{64,96},{96,128},{128,160},{160,192},{192,224},{224... | collective-permute-start | bytes 983048 | tf_op jit(solution)/shard_map/ppermute | solution.py:369
  7.7 4.0 %shard_map.140 = (bf16[2,128,640]{2,1,0:T(8,128)(2,1)S(1)}, bf16[960,960]{1,0:T(8,128)(2,1)S(1)}, bf16[960,960]{1,0:T(8,128)(2,1)S(1)}, bf16[1024,320]{1,0:T(8,128)(2,1)}) custom-call(bf16[512,320]{1,0:T(8,128)(2,1)S(1)} %get-tuple-element.25.current, bf16[1024,320]{1,0:T(8,128)(2,1)S(1)} %get-tuple-element.24.skips, ...), custom_call_target="tpu_custom_call" | custom-call | tf_op jit(solution)/shard_map/pallas_call | solution.py:103
  11.7 2.9 %collective-permute-start.1 = (bf16[2,128,640]{2,1,0:T(8,128)(2,1)S(1)}, bf16[2,128,640]{2,1,0:T(8,128)(2,1)S(1)}, u32[]{:S(2)}, u32[]{:S(2)}) collective-permute-start(bf16[2,128,640]{2,1,0:T(8,128)(2,1)S(1)} %get-tuple-element.36.early), channel_id=1, source_target_pairs={{0,32},{32,64},{64,96},{96,128},{128,160},{160,192},{192,224},{1,3... | collective-permute-start | bytes 983048 | tf_op jit(solution)/shard_map/ppermute | solution.py:371
  14.7 1.5 %collective-permute-done.moved.moved_enc = bf16[2,128,640]{2,1,0:T(8,128)(2,1)S(1)} collective-permute-done((bf16[2,128,640]{2,1,0:T(8,128)(2,1)S(1)}, bf16[2,128,640]{2,1,0:T(8,128)(2,1)S(1)}, u32[]{:S(2)}, u32[]{:S(2)}) %collective-permute-start) | collective-permute-done | bytes 327712 | tf_op jit(solution)/shard_map/ppermute | solution.py:369
  16.2 2.5 %shard_map.141 = (bf16[2,128,640]{2,1,0:T(8,128)(2,1)S(1)}, bf16[1024,320]{1,0:T(8,128)(2,1)}) custom-call(bf16[512,320]{1,0:T(8,128)(2,1)S(1)} %get-tuple-element.31.fresh, bf16[2,128,640]{2,1,0:T(8,128)(2,1)S(1)} %collective-permute-done.moved.moved_enc, bf16[960,960]{1,0:T(8,128)(2,1)S(1)} %get-tuple-element.32.taps, ...), custom_call_target="tpu_custom_call" | custom-call | tf_op jit(solution)/shard_map/pallas_call | solution.py:103
  18.7 2.7 %collective-permute-start.3 = (bf16[2,128,640]{2,1,0:T(8,128)(2,1)S(1)}, bf16[2,128,640]{2,1,0:T(8,128)(2,1)S(1)}, u32[]{:S(2)}, u32[]{:S(2)}) collective-permute-start(bf16[2,128,640]{2,1,0:T(8,128)(2,1)S(1)} %get-tuple-element.37.late), channel_id=1, source_target_pairs={{0,224},{32,192},{64,160},{96,128},{128,96},{160,64},{192,32},{224... | collective-permute-start | bytes 983048 | tf_op jit(solution)/shard_map/ppermute | solution.py:374
  21.4 2.9 %collective-permute-start.2 = (bf16[2,128,640]{2,1,0:T(8,128)(2,1)S(1)}, bf16[2,128,640]{2,1,0:T(8,128)(2,1)S(1)}, u32[]{:S(2)}, u32[]{:S(2)}) collective-permute-start(bf16[2,128,640]{2,1,0:T(8,128)(2,1)S(1)} %collective-permute-done.moved.moved_enc), channel_id=1, source_target_pairs={{32,224},{64,192},{96,160},{160,96},{192,64},{224,32},{33,225},{65... | collective-permute-start | bytes 983048 | tf_op jit(solution)/shard_map/ppermute | solution.py:372
  24.3 2.6 %shard_map.142 = (f32[512,320]{1,0:T(8,128)S(1)}, bf16[1024,320]{1,0:T(8,128)(2,1)}) custom-call(bf16[2,128,640]{2,1,0:T(8,128)(2,1)S(1)} %collective-permute-done.moved.moved_enc, bf16[1024,320]{1,0:T(8,128)(2,1)S(1)} %get-tuple-element.24.skips, bf16[960,960]{1,0:T(8,128)(2,1)S(1)} %get-tuple-element.30.taps, ...), custom_call_target="tpu_custom_call", output_to_operand_aliasing={{1}: (7, {})} | custom-call | tf_op jit(solution)/shard_map/pallas_call | solution.py:103
  26.9 0.0 collective-permute-done.1.moved_dec
  26.9 2.9 %shard_map.143 = bf16[1024,320]{1,0:T(8,128)(2,1)} custom-call(bf16[2,128,640]{2,1,0:T(8,128)(2,1)S(1)} %collective-permute-done.moved.moved_enc, bf16[2,128,640]{2,1,0:T(8,128)(2,1)S(1)} %collective-permute-done.1.moved_dec, bf16[960,960]{1,0:T(8,128)(2,1)S(1)} %get-tuple-element.40.taps, ...), custom_call_target="tpu_custom_call", output_to_operand_aliasing={{}: (6, {})} | custom-call | tf_op jit(solution)/shard_map/pallas_call | solution.py:103
  29.8 7.3 %collective-permute-done.3.last = bf16[2,128,640]{2,1,0:T(8,128)(2,1)S(1)} collective-permute-done((bf16[2,128,640]{2,1,0:T(8,128)(2,1)S(1)}, bf16[2,128,640]{2,1,0:T(8,128)(2,1)S(1)}, u32[]{:S(2)}, u32[]{:S(2)}) %collective-permute-start.3) | collective-permute-done | bytes 327712 | tf_op jit(solution)/shard_map/ppermute | solution.py:374
  37.1 1.1 %collective-permute-done.2.turned = bf16[2,128,640]{2,1,0:T(8,128)(2,1)S(1)} collective-permute-done((bf16[2,128,640]{2,1,0:T(8,128)(2,1)S(1)}, bf16[2,128,640]{2,1,0:T(8,128)(2,1)S(1)}, u32[]{:S(2)}, u32[]{:S(2)}) %collective-permute-start.2) | collective-permute-done | bytes 327712 | tf_op jit(solution)/shard_map/ppermute | solution.py:372
  38.2 1.0 %shard_map.144 = bf16[1024,320]{1,0:T(8,128)(2,1)} custom-call(bf16[2,128,640]{2,1,0:T(8,128)(2,1)S(1)} %collective-permute-done.2.turned, bf16[2,128,640]{2,1,0:T(8,128)(2,1)S(1)} %collective-permute-done.moved.moved_enc, bf16[2,128,640]{2,1,0:T(8,128)(2,1)S(1)} %collective-permute-done.3.last), custom_call_target="tpu_custom_call" | custom-call | tf_op jit(solution)/shard_map/pallas_call | solution.py:103
Async XLA Ops:
  5.8 10.4 %collective-permute-start = (bf16[2,128,640]{2,1,0:T(8,128)(2,1)S(1)}, bf16[2,128,640]{2,1,0:T(8,128)(2,1)S(1)}, u32[]{:S(2)}, u32[]{:S(2)}) collective-permute-start(bf16[2,128,640]{2,1,0:T(8,128)(2,1)S(1)} %get-tuple-element.23.early), channel_id=1, source_target_pairs={{0,32},{32,64},{64,96},{96,128},{128,160},{160,192},{192,224},{224... | collective-permute-start | bytes 983048 | tf_op jit(solution)/shard_map/ppermute | solution.py:369
  11.7 15.2 %collective-permute-start.1 = (bf16[2,128,640]{2,1,0:T(8,128)(2,1)S(1)}, bf16[2,128,640]{2,1,0:T(8,128)(2,1)S(1)}, u32[]{:S(2)}, u32[]{:S(2)}) collective-permute-start(bf16[2,128,640]{2,1,0:T(8,128)(2,1)S(1)} %get-tuple-element.36.early), channel_id=1, source_target_pairs={{0,32},{32,64},{64,96},{96,128},{128,160},{160,192},{192,224},{1,3... | collective-permute-start | bytes 983048 | tf_op jit(solution)/shard_map/ppermute | solution.py:371
  18.7 18.4 %collective-permute-start.3 = (bf16[2,128,640]{2,1,0:T(8,128)(2,1)S(1)}, bf16[2,128,640]{2,1,0:T(8,128)(2,1)S(1)}, u32[]{:S(2)}, u32[]{:S(2)}) collective-permute-start(bf16[2,128,640]{2,1,0:T(8,128)(2,1)S(1)} %get-tuple-element.37.late), channel_id=1, source_target_pairs={{0,224},{32,192},{64,160},{96,128},{128,96},{160,64},{192,32},{224... | collective-permute-start | bytes 983048 | tf_op jit(solution)/shard_map/ppermute | solution.py:374
  21.4 16.8 %collective-permute-start.2 = (bf16[2,128,640]{2,1,0:T(8,128)(2,1)S(1)}, bf16[2,128,640]{2,1,0:T(8,128)(2,1)S(1)}, u32[]{:S(2)}, u32[]{:S(2)}) collective-permute-start(bf16[2,128,640]{2,1,0:T(8,128)(2,1)S(1)} %collective-permute-done.moved.moved_enc), channel_id=1, source_target_pairs={{32,224},{64,192},{96,160},{160,96},{192,64},{224,32},{33,225},{65... | collective-permute-start | bytes 983048 | tf_op jit(solution)/shard_map/ppermute | solution.py:372

commit v3 on v2

--- a/solution.py
+++ b/solution.py
@@ -107,7 +107,7 @@
         out_specs=tuple(HBM if isinstance(out, jax.ShapeDtypeStruct) else VMEM for out in outputs),
         scratch_shapes=list(scratch),
         input_output_aliases=aliases or {},
-        compiler_params=pltpu.CompilerParams(vmem_limit_bytes=16 * 2**20),
+        compiler_params=pltpu.CompilerParams(vmem_limit_bytes=24 * 2**20),
     )(*held)
 
 
@@ -138,13 +138,15 @@
         first.append(begin(beta, beta_near, sems.at[2]))
         first.append(begin(bias, bias_near, sems.at[3]))
         weights = [begin(weight.at[ky], kernel.at[ky], sems.at[4 + ky]) for ky in range(3)]
-        fetched = [begin(far[k], close[k], later_sems.at[k]) for k in range(count)]
+        fetched = []
         for copy in first:
             copy.wait()
 
         def ready():
+            for copy in weights:
+                copy.wait()
+            fetched.extend(begin(far[k], close[k], later_sems.at[k]) for k in range(count))
             for ky in range(3):
-                weights[ky].wait()
                 taps[pl.ds(ky * C, C)] = jnp.concatenate([kernel[ky, kx] for kx in range(3)], axis=1)
 
         enc_rest(current, gain_near, beta_near, bias_near, taps, wide, sums, send, ready)
@@ -208,114 +210,114 @@
     return lax.dot_general(wide[...], taps[...], (((1,), (1,)), ((), ())), preferred_element_type=F32)
 
 
-def dec_first(current, skips, kernel, dec_rows, enc_sent):
-    def body(current, skips, kernel, bias, gain, beta, early, send, near, far, encoded, *scratch):
-        wide, sums, result, sems = scratch
-        taps = (near, far)
+def dec_first(current, skips, weight, dec_rows, enc_sent):
+    def body(current, skips, weight, bias, gain, beta, early, send, near, far, part, encoded, *scratch):
+        kernel, wide, sums, ahead, result, sems = scratch
+        weights = [begin(weight.at[ky], kernel.at[ky], sems.at[IMAGES + ky]) for ky in range(3)]
         copies = write_maps(early, result, encoded, sems, 0, 0)
-        loads = [lambda m=m, i=i: m[image(i)] for m in (current, skips) for i in range(IMAGES)]
-        gains = [gain[:, :C]] * IMAGES + [gain[:, C:]] * IMAGES
-        betas = [beta[:, :C]] * IMAGES + [beta[:, C:]] * IMAGES
+        starts = ((current, 0), (skips, 0), (skips, ROWS))
+        loads = [lambda m=m, i=i, base=base: m[image(i, base)] for m, base in starts for i in range(IMAGES)]
+        gains = [gain[:, :C]] * IMAGES + [gain[:, C:]] * (2 * IMAGES)
+        betas = [beta[:, :C]] * IMAGES + [beta[:, C:]] * (2 * IMAGES)
         hidden = norm_all(loads, gains, betas, 2 * C // GROUPS)
-        for part in range(2):
+        for source in range(3):
             for i in range(IMAGES):
-                wide[part, image(i)] = spread_rows(hidden[part * IMAGES + i])
-            cut = slice(part * C, (part + 1) * C)
-            taps[part][...] = jnp.concatenate([kernel[ky, :, cut] for ky in range(3)], axis=1)
+                wide[source, image(i)] = spread_rows(hidden[source * IMAGES + i])
+        for copy in weights:
+            copy.wait()
+        for half, taps in enumerate((near, far)):
+            cut = slice(half * C, (half + 1) * C)
+            taps[...] = jnp.concatenate([kernel[ky, :, cut] for ky in range(3)], axis=1)
         sums[...] = multiply(wide.at[0], near) + multiply(wide.at[1], far)
         for i in range(IMAGES):
             total = current[image(i)].astype(F32) + gather_columns(sums[image(i)]) + bias[...]
             send[i] = pack(total.astype(BF16))
+        ahead[...] = multiply(wide.at[2], far)
+        for i in range(IMAGES):
+            part[image(i)] = gather_columns(ahead[image(i)]) + bias[...]
         for copy in copies:
             copy.wait()
 
     return call(
         body,
-        (current, skips, kernel) + tuple(dec_rows) + (enc_sent,),
-        [VMEM] * 7,
-        [pltpu.VMEM(PARCEL, BF16), pltpu.VMEM((TAPS, TAPS), BF16), pltpu.VMEM((TAPS, TAPS), BF16), WHOLE],
-        [
-            pltpu.VMEM((2, ROWS, TAPS), BF16),
-            pltpu.VMEM((ROWS, TAPS), F32),
-            pltpu.VMEM((ROWS, C), BF16),
-            pltpu.SemaphoreType.DMA((IMAGES,)),
-        ],
-    )
-
-
-def dec_skip(moved_enc, skips, taps, dec_rows, last_sent, encoded):
-    def body(moved, skips, taps, bias, gain, beta, late, _, part, encoded, *scratch):
-        result, skipped, wide, sums, sems = scratch
-        copies = write_maps(late, result, encoded, sems, ROWS, 0)
-        leading = lax.axis_index("section") == 0
-        for i in range(IMAGES):
-            skipped[image(i)] = jnp.where(leading, unpack(moved[i]), skips[image(i, ROWS)])
-        loads = [lambda i=i: skipped[image(i)] for i in range(IMAGES)]
-        hidden = norm_all(loads, [gain[:, C:]] * IMAGES, [beta[:, C:]] * IMAGES, 2 * C // GROUPS)
-        for i in range(IMAGES):
-            wide[image(i)] = spread_rows(hidden[i])
-        sums[...] = multiply(wide, taps)
-        for i in range(IMAGES):
-            part[image(i)] = gather_columns(sums[image(i)]) + bias[...]
-        for copy in copies:
-            copy.wait()
-
-    return call(
-        body,
-        (moved_enc, skips, taps) + tuple(dec_rows) + (last_sent, encoded),
-        [VMEM] * 7 + [HBM],
-        [pltpu.VMEM((ROWS, C), F32), WHOLE],
-        [
-            pltpu.VMEM((ROWS, C), BF16),
-            pltpu.VMEM((ROWS, C), BF16),
-            pltpu.VMEM((ROWS, TAPS), BF16),
-            pltpu.VMEM((ROWS, TAPS), F32),
-            pltpu.SemaphoreType.DMA((IMAGES,)),
-        ],
-        {7: 1},
-    )
-
-
-def dec_second(moved_enc, moved_dec, taps, part, dec_rows, decoded):
-    def body(moved_enc, moved_dec, taps, part, gain, beta, _, out, *scratch):
-        current, wide, sums, result, sems = scratch
+        (current, skips, weight) + tuple(dec_rows) + (enc_sent,),
+        [VMEM, VMEM, HBM] + [VMEM] * 4,
+        [
+            pltpu.VMEM(PARCEL, BF16),
+            pltpu.VMEM((TAPS, TAPS), BF16),
+            pltpu.VMEM((TAPS, TAPS), BF16),
+            pltpu.VMEM((ROWS, C), F32),
+            WHOLE,
+        ],
+        [
+            pltpu.VMEM((3, TAPS, 2 * C), BF16),
+            pltpu.VMEM((3, ROWS, TAPS), BF16),
+            pltpu.VMEM((ROWS, TAPS), F32),
+            pltpu.VMEM((ROWS, TAPS), F32),
+            pltpu.VMEM((ROWS, C), BF16),
+            pltpu.SemaphoreType.DMA((IMAGES + 3,)),
+        ],
+    )
+
+
+def dec_second(moved_enc, moved_dec, near, far, part, dec_rows, last_sent, encoded, decoded):
+    def body(moved_enc, moved_dec, near, far, part, bias, gain, beta, late, _, __, encoded, decoded, *scratch):
+        current, wide, sums, skip_part, written, result, sems = scratch
+        copies = write_maps(late, written, encoded, sems, ROWS, 0)
         leading = lax.axis_index("section") == 0
         for i in range(IMAGES):
             current[image(i)] = unpack(jnp.where(leading, moved_enc[i], moved_dec[i]))
         loads = [lambda i=i: current[image(i)] for i in range(IMAGES)]
-        hidden = norm_all(loads, [gain[:, :C]] * IMAGES, [beta[:, :C]] * IMAGES, 2 * C // GROUPS)
-        for i in range(IMAGES):
-            wide[image(i)] = spread_rows(hidden[i])
-        sums[...] = multiply(wide, taps)
-        copies = []
-        for i in range(IMAGES):
-            total = current[image(i)].astype(F32) + gather_columns(sums[image(i)]) + part[image(i)]
+
+        def product(half, taps):
+            cut = slice(half * C, (half + 1) * C)
+            hidden = norm_all(loads, [gain[:, cut]] * IMAGES, [beta[:, cut]] * IMAGES, 2 * C // GROUPS)
+            for i in range(IMAGES):
+                wide[image(i)] = spread_rows(hidden[i])
+            sums[...] = multiply(wide, taps)
+
+        @pl.when(leading)
+        def _():
+            product(1, far)
+            for i in range(IMAGES):
+                skip_part[image(i)] = gather_columns(sums[image(i)]) + bias[...]
+
+        @pl.when(jnp.logical_not(leading))
+        def _():
+            skip_part[...] = part[...]
+
+        product(0, near)
+        for i in range(IMAGES):
+            total = current[image(i)].astype(F32) + gather_columns(sums[image(i)]) + skip_part[image(i)]
             result[image(i)] = total.astype(BF16)
-            copies.append(begin(result.at[image(i)], out.at[image(i, ROWS)], sems.at[i]))
+            copies.append(begin(result.at[image(i)], decoded.at[image(i, ROWS)], sems.at[IMAGES + i]))
         for copy in copies:
             copy.wait()
 
     return call(
         body,
-        (moved_enc, moved_dec, taps, part, dec_rows[1], dec_rows[2], decoded),
-        [VMEM] * 6 + [HBM],
-        [WHOLE],
+        (moved_enc, moved_dec, near, far, part) + tuple(dec_rows) + (last_sent, encoded, decoded),
+        [VMEM] * 9 + [HBM, HBM],
+        [WHOLE, WHOLE],
         [
             pltpu.VMEM((ROWS, C), BF16),
             pltpu.VMEM((ROWS, TAPS), BF16),
             pltpu.VMEM((ROWS, TAPS), F32),
-            pltpu.VMEM((ROWS, C), BF16),
-            pltpu.SemaphoreType.DMA((IMAGES,)),
-        ],
-        {6: 0},
-    )[0]
-
-
-def queue_maps(turned, moved, last):
-    def body(turned, moved, last, out, chosen, result, sems):
+            pltpu.VMEM((ROWS, C), F32),
+            pltpu.VMEM((ROWS, C), BF16),
+            pltpu.VMEM((ROWS, C), BF16),
+            pltpu.SemaphoreType.DMA((2 * IMAGES,)),
+        ],
+        {9: 0, 10: 1},
+    )
+
+
+def queue_maps(direct, turned, moved, last):
+    def body(direct, turned, moved, last, out, chosen, result, sems):
         shared = lax.axis_index("section") % 4 == 0
-        for i in range(IMAGES):
-            chosen[i] = jnp.where(shared, moved[i], turned[i])
+        first = lax.axis_index("dp") % 2 == 0
+        for i in range(IMAGES):
+            chosen[i] = jnp.where(shared, moved[i], jnp.where(first, direct[i], turned[i]))
         copies = write_maps(chosen, result, out, sems, 0, 0)
         copies += write_maps(last, result, out, sems, ROWS, 1)
         for copy in copies:
@@ -323,8 +325,8 @@
 
     return call(
         body,
-        (turned, moved, last),
-        [VMEM, VMEM, VMEM],
+        (direct, turned, moved, last),
+        [VMEM, VMEM, VMEM, VMEM],
         [WHOLE],
         [
             pltpu.VMEM(PARCEL, BF16),
@@ -350,13 +352,14 @@
 ):
     forward = [(s, (s + 1) % 8) for s in range(8)]
     mirror = [(s, 7 - s) for s in range(8)]
-    relay = [(s, 8 - s) for s in range(1, 8) if s != 4]
+    groups = lax.axis_size("dp")
+    direct = [(groups * s + g, groups * (7 - s) + g) for g in range(0, groups, 2) for s in range(8) if s % 4 != 3]
+    relay = [(groups * s + g, groups * (8 - s) + g) for g in range(1, groups, 2) for s in range(8) if s % 4]
     enc_kernel = enc_weight.reshape(3, 3, C, C)
     dec_kernel = jnp.transpose(dec_weight, (0, 1, 2, 4, 3)).reshape(3, TAPS, 2 * C)
     later = (
         dec_in.reshape(ROWS, C),
         skip_queue.reshape(TICKS * ROWS, C),
-        dec_kernel,
         dec_bias,
         dec_gain,
         dec_beta,
@@ -365,16 +368,18 @@
     enc_sent, enc_taps, *held = enc_first(
         enc_in.reshape(ROWS, C), enc_kernel, (enc_bias, enc_gain, enc_beta), later
     )
-    enc_rows, (dec_now, skips, dec_kernel), dec_rows, fresh_now = held[:3], held[3:6], held[6:9], held[9]
+    enc_rows, (dec_now, skips), dec_rows, fresh_now = held[:3], held[3:5], held[5:8], held[8]
     moved_enc = lax.ppermute(enc_sent, "section", forward)
-    dec_sent, dec_taps, skip_taps, encoded = dec_first(dec_now, skips, dec_kernel, dec_rows, enc_sent)
+    turned_direct = lax.ppermute(enc_sent, ("section", "dp"), direct)
+    dec_sent, near, far, part, encoded = dec_first(dec_now, skips, dec_kernel, dec_rows, enc_sent)
+    turned = lax.ppermute(moved_enc, ("section", "dp"), relay)
     moved_dec = lax.ppermute(dec_sent, "section", [pair for pair in forward if pair[1] != 0])
-    turned = lax.ppermute(moved_enc, "section", relay)
     last_sent, decoded = enc_second(fresh_now, moved_enc, enc_taps, enc_rows, dec_sent)
     last = lax.ppermute(last_sent, "section", mirror)
-    part, encoded = dec_skip(moved_enc, skips, skip_taps, dec_rows, last_sent, encoded)
-    decoded = dec_second(moved_enc, moved_dec, dec_taps, part, dec_rows, decoded)
-    queued = queue_maps(turned, moved_enc, last)
+    encoded, decoded = dec_second(
+        moved_enc, moved_dec, near, far, part, dec_rows, last_sent, encoded, decoded
+    )
+    queued = queue_maps(turned_direct, turned, moved_enc, last)
     shape = (TICKS * IMAGES, SIDE, SIDE, C)
     return encoded.reshape(shape), decoded.reshape(shape), queued.reshape(shape)
 

time: 40 us -> 36.7 us (0.918)
  waiting for transfers between devices: 9.88 us -> 7.54 us
  Pallas kernels: 18.1 us -> 16.5 us
  starting transfers between devices: 10.6 us -> 11.1 us
    ppermute x1, waiting for transfers between devices: 0.01 us -> 4.92 us  [shards(): lax.ppermute(dec_sent, 'section', [pair for pair in forward if pair[1] !=...]
    ppermute x1, waiting for transfers between devices: 7.27 us -> 2.61 us  [shards(): last = lax.ppermute(last_sent, 'section', mirror)]
    pallas_call x6 -> x5, Pallas kernels: 18.1 us -> 16.5 us  [call(): pl.pallas_call(body, out_shape=tuple(outputs), in_specs=list(in_specs), o...]
    ppermute x1, waiting for transfers between devices: 1.5 us -> 0.01 us  [shards(): moved_enc = lax.ppermute(enc_sent, 'section', forward)]
    ppermute x1 -> x2, starting transfers between devices: 2.89 us -> 4.24 us  [the longest x1 3.57 us: shards(): turned_direct = lax.ppermute(enc_sent, ('section', 'dp'), direct)]
    ppermute x1 -> x2, waiting for transfers between devices: 1.1 us -> 0.01 us  [the longest x1 0.01 us: shards(): turned = lax.ppermute(moved_enc, ('section', 'dp'), relay)]
    ppermute x1, starting transfers between devices: 2.95 us -> 1.92 us  [shards(): lax.ppermute(dec_sent, 'section', [pair for pair in forward if pair[1] !=...]
  transfers between devices with their start and end apart: 4 -> 5, of which waited for: 3 -> 2; matrix products, arithmetic and copies ran while one was open for 0% -> 0% of each run, Pallas kernels for 30% -> 33%
where the time goes in v3:
time: 36.7 us; the launch traced here: 36 us
  Pallas kernels  16.5 us (45%)
  starting transfers between devices  11.1 us (30%)
  waiting for transfers between devices  7.54 us (21%)
  between operations  0.87 us (2%)
    pallas_call x5, Pallas kernels, call(): pl.pallas_call(body, out_shape=tuple(outputs), in_specs=list(in_specs), o...  16.5 us
    ppermute x1, waiting for transfers between devices, shards(): lax.ppermute(dec_sent, 'section', [pair for pair in forward if pair[1] !=...  4.92 us
    ppermute x1, starting transfers between devices, shards(): turned_direct = lax.ppermute(enc_sent, ('section', 'dp'), direct)  3.57 us
    ppermute x1, starting transfers between devices, shards(): last = lax.ppermute(last_sent, 'section', mirror)  2.95 us
    ppermute x1, waiting for transfers between devices, shards(): last = lax.ppermute(last_sent, 'section', mirror)  2.61 us
    ppermute x1, starting transfers between devices, shards(): moved_enc = lax.ppermute(enc_sent, 'section', forward)  1.99 us
    ppermute x1, starting transfers between devices, shards(): lax.ppermute(dec_sent, 'section', [pair for pair in forward if pair[1] !=...  1.92 us
  transfers between devices with their start and end apart: 5, of which 2 were waited for; matrix products, arithmetic and copies ran while one was open for 0% of the time, Pallas kernels for 33%

profile of v3, /device:TPU:82, one launch (start us, length us, event | category | flops | bytes accessed | tf_op | source)
XLA Modules:
  0.0 36.0 jit_solution(15557454477241734264)
XLA Ops:
  0.6 3.6 %shard_map.139 = (bf16[2,128,640]{2,1,0:T(8,128)(2,1)S(1)}, bf16[960,960]{1,0:T(8,128)(2,1)S(1)}, f32[1,320]{1,0:T(1,128)S(1)}, f32[1,320]{1,0:T(1,128)S(1)}, f3...) custom-call(bf16[512,320]{1,0:T(8,128)(2,1)} %bitcast.17, ...), custom_call_target="tpu_custom_call" | custom-call | tf_op jit(solution)/shard_map/pallas_call | solution.py:103
  4.2 2.0 %collective-permute-start = (bf16[2,128,640]{2,1,0:T(8,128)(2,1)S(1)}, bf16[2,128,640]{2,1,0:T(8,128)(2,1)S(1)}, u32[]{:S(2)}, u32[]{:S(2)}) collective-permute-start(bf16[2,128,640]{2,1,0:T(8,128)(2,1)S(1)} %get-tuple-element.23.early), channel_id=1, source_target_pairs={{0,32},{32,64},{64,96},{96,128},{128,160},{160,192},{192,224},{224... | collective-permute-start | bytes 983048 | tf_op jit(solution)/shard_map/ppermute | solution.py:372
  6.2 3.6 %collective-permute-start.2 = (bf16[2,128,640]{2,1,0:T(8,128)(2,1)S(1)}, bf16[2,128,640]{2,1,0:T(8,128)(2,1)S(1)}, u32[]{:S(2)}, u32[]{:S(2)}) collective-permute-start(bf16[2,128,640]{2,1,0:T(8,128)(2,1)S(1)} %get-tuple-element.23.early), channel_id=1, source_target_pairs={{0,224},{32,192},{64,160},{128,96},{160,64},{192,32},{2,226},{34,1... | collective-permute-start | bytes 983048 | tf_op jit(solution)/shard_map/ppermute | solution.py:373
  9.8 6.2 %shard_map.140 = (bf16[2,128,640]{2,1,0:T(8,128)(2,1)S(1)}, bf16[960,960]{1,0:T(8,128)(2,1)S(1)}, bf16[960,960]{1,0:T(8,128)(2,1)S(1)}, f32[512,320]{1,0:T(8,128)S(1)}, bf16[1024,320]{1,0:T(8,128)(2,1)}) custom-call(bf16[512,320]{1,0:T(8,128)(2,1)S(1)} %get-tuple-element.24.current, bf16[1024,320]{1,0:T(8,128)(2,1)S(1)} %get-tuple-element.25.skips, ...), custom_call_target="tpu_custom_call" | custom-call | tf_op jit(solution)/shard_map/pallas_call | solution.py:103
  16.0 1.9 %collective-permute-start.1 = (bf16[2,128,640]{2,1,0:T(8,128)(2,1)S(1)}, bf16[2,128,640]{2,1,0:T(8,128)(2,1)S(1)}, u32[]{:S(2)}, u32[]{:S(2)}) collective-permute-start(bf16[2,128,640]{2,1,0:T(8,128)(2,1)S(1)} %get-tuple-element.29.early), channel_id=1, source_target_pairs={{0,32},{32,64},{64,96},{96,128},{128,160},{160,192},{192,224},{1,3... | collective-permute-start | bytes 983048 | tf_op jit(solution)/shard_map/ppermute | solution.py:376
  17.9 0.0 collective-permute-done.moved.moved_enc
  17.9 2.5 %shard_map.141 = (bf16[2,128,640]{2,1,0:T(8,128)(2,1)S(1)}, bf16[1024,320]{1,0:T(8,128)(2,1)}) custom-call(bf16[512,320]{1,0:T(8,128)(2,1)S(1)} %get-tuple-element.33.fresh, bf16[2,128,640]{2,1,0:T(8,128)(2,1)S(1)} %collective-permute-done.moved.moved_enc, bf16[960,960]{1,0:T(8,128)(2,1)S(1)} %get-tuple-element.34.taps, ...), custom_call_target="tpu_custom_call" | custom-call | tf_op jit(solution)/shard_map/pallas_call | solution.py:103
  20.4 3.0 %collective-permute-start.4 = (bf16[2,128,640]{2,1,0:T(8,128)(2,1)S(1)}, bf16[2,128,640]{2,1,0:T(8,128)(2,1)S(1)}, u32[]{:S(2)}, u32[]{:S(2)}) collective-permute-start(bf16[2,128,640]{2,1,0:T(8,128)(2,1)S(1)} %get-tuple-element.38.late), channel_id=1, source_target_pairs={{0,224},{32,192},{64,160},{96,128},{128,96},{160,64},{192,32},{224... | collective-permute-start | bytes 983048 | tf_op jit(solution)/shard_map/ppermute | solution.py:378
  23.4 0.7 %collective-permute-start.3 = (bf16[2,128,640]{2,1,0:T(8,128)(2,1)S(1)}, bf16[2,128,640]{2,1,0:T(8,128)(2,1)S(1)}, u32[]{:S(2)}, u32[]{:S(2)}) collective-permute-start(bf16[2,128,640]{2,1,0:T(8,128)(2,1)S(1)} %collective-permute-done.moved.moved_enc), channel_id=1, source_target_pairs={{33,225},{65,193},{97,161},{161,97},{193,65},{225,33},{35,227},{67... | collective-permute-start | bytes 983048 | tf_op jit(solution)/shard_map/ppermute | solution.py:375
  24.0 4.9 %collective-permute-done.1.moved_dec = bf16[2,128,640]{2,1,0:T(8,128)(2,1)S(1)} collective-permute-done((bf16[2,128,640]{2,1,0:T(8,128)(2,1)S(1)}, bf16[2,128,640]{2,1,0:T(8,128)(2,1)S(1)}, u32[]{:S(2)}, u32[]{:S(2)}) %collective-permute-start.1) | collective-permute-done | bytes 327712 | tf_op jit(solution)/shard_map/ppermute | solution.py:376
  29.0 3.2 %shard_map.142 = (bf16[1024,320]{1,0:T(8,128)(2,1)}, bf16[1024,320]{1,0:T(8,128)(2,1)}) custom-call(bf16[2,128,640]{2,1,0:T(8,128)(2,1)S(1)} %collective-permute-done.moved.moved_enc, bf16[2,128,640]{2,1,0:T(8,128)(2,1)S(1)} %collective-permute-done.1.moved_dec, ...), custom_call_target="tpu_custom_call", output_to_operand_aliasing={{0}: (9, {}), {1}: (10, {})} | custom-call | tf_op jit(solution)/shard_map/pallas_call | solution.py:103
  32.2 0.0 collective-permute-done.2.direct
  32.2 2.6 %collective-permute-done.4.last = bf16[2,128,640]{2,1,0:T(8,128)(2,1)S(1)} collective-permute-done((bf16[2,128,640]{2,1,0:T(8,128)(2,1)S(1)}, bf16[2,128,640]{2,1,0:T(8,128)(2,1)S(1)}, u32[]{:S(2)}, u32[]{:S(2)}) %collective-permute-start.4) | collective-permute-done | bytes 327712 | tf_op jit(solution)/shard_map/ppermute | solution.py:378
  34.8 0.0 collective-permute-done.3.turned
  34.8 1.0 %shard_map.143 = bf16[1024,320]{1,0:T(8,128)(2,1)} custom-call(bf16[2,128,640]{2,1,0:T(8,128)(2,1)S(1)} %collective-permute-done.2.direct, bf16[2,128,640]{2,1,0:T(8,128)(2,1)S(1)} %collective-permute-done.3.turned, bf16[2,128,640]{2,1,0:T(8,128)(2,1)S(1)} %collective-permute-done.moved.moved_enc, bf16[2,128,640]{2,1,0:T(8,128)(2,1)S(1)} %collective-permute-done.4.last), custom_call_target="tpu_custom_call" | custom-call | tf_op jit(solution)/shard_map/pallas_call | solution.py:103
Async XLA Ops:
  4.2 13.7 %collective-permute-start = (bf16[2,128,640]{2,1,0:T(8,128)(2,1)S(1)}, bf16[2,128,640]{2,1,0:T(8,128)(2,1)S(1)}, u32[]{:S(2)}, u32[]{:S(2)}) collective-permute-start(bf16[2,128,640]{2,1,0:T(8,128)(2,1)S(1)} %get-tuple-element.23.early), channel_id=1, source_target_pairs={{0,32},{32,64},{64,96},{96,128},{128,160},{160,192},{192,224},{224... | collective-permute-start | bytes 983048 | tf_op jit(solution)/shard_map/ppermute | solution.py:372
  6.2 26.0 %collective-permute-start.2 = (bf16[2,128,640]{2,1,0:T(8,128)(2,1)S(1)}, bf16[2,128,640]{2,1,0:T(8,128)(2,1)S(1)}, u32[]{:S(2)}, u32[]{:S(2)}) collective-permute-start(bf16[2,128,640]{2,1,0:T(8,128)(2,1)S(1)} %get-tuple-element.23.early), channel_id=1, source_target_pairs={{0,224},{32,192},{64,160},{128,96},{160,64},{192,32},{2,226},{34,1... | collective-permute-start | bytes 983048 | tf_op jit(solution)/shard_map/ppermute | solution.py:373
  16.0 13.0 %collective-permute-start.1 = (bf16[2,128,640]{2,1,0:T(8,128)(2,1)S(1)}, bf16[2,128,640]{2,1,0:T(8,128)(2,1)S(1)}, u32[]{:S(2)}, u32[]{:S(2)}) collective-permute-start(bf16[2,128,640]{2,1,0:T(8,128)(2,1)S(1)} %get-tuple-element.29.early), channel_id=1, source_target_pairs={{0,32},{32,64},{64,96},{96,128},{128,160},{160,192},{192,224},{1,3... | collective-permute-start | bytes 983048 | tf_op jit(solution)/shard_map/ppermute | solution.py:376
  20.4 14.4 %collective-permute-start.4 = (bf16[2,128,640]{2,1,0:T(8,128)(2,1)S(1)}, bf16[2,128,640]{2,1,0:T(8,128)(2,1)S(1)}, u32[]{:S(2)}, u32[]{:S(2)}) collective-permute-start(bf16[2,128,640]{2,1,0:T(8,128)(2,1)S(1)} %get-tuple-element.38.late), channel_id=1, source_target_pairs={{0,224},{32,192},{64,160},{96,128},{128,96},{160,64},{192,32},{224... | collective-permute-start | bytes 983048 | tf_op jit(solution)/shard_map/ppermute | solution.py:378
  23.4 11.4 %collective-permute-start.3 = (bf16[2,128,640]{2,1,0:T(8,128)(2,1)S(1)}, bf16[2,128,640]{2,1,0:T(8,128)(2,1)S(1)}, u32[]{:S(2)}, u32[]{:S(2)}) collective-permute-start(bf16[2,128,640]{2,1,0:T(8,128)(2,1)S(1)} %collective-permute-done.moved.moved_enc), channel_id=1, source_target_pairs={{33,225},{65,193},{97,161},{161,97},{193,65},{225,33},{35,227},{67... | collective-permute-start | bytes 983048 | tf_op jit(solution)/shard_map/ppermute | solution.py:375

commit v4 on v2

--- a/solution.py
+++ b/solution.py
@@ -107,7 +107,7 @@
         out_specs=tuple(HBM if isinstance(out, jax.ShapeDtypeStruct) else VMEM for out in outputs),
         scratch_shapes=list(scratch),
         input_output_aliases=aliases or {},
-        compiler_params=pltpu.CompilerParams(vmem_limit_bytes=16 * 2**20),
+        compiler_params=pltpu.CompilerParams(vmem_limit_bytes=24 * 2**20),
     )(*held)
 
 
@@ -138,13 +138,15 @@
         first.append(begin(beta, beta_near, sems.at[2]))
         first.append(begin(bias, bias_near, sems.at[3]))
         weights = [begin(weight.at[ky], kernel.at[ky], sems.at[4 + ky]) for ky in range(3)]
-        fetched = [begin(far[k], close[k], later_sems.at[k]) for k in range(count)]
+        fetched = []
         for copy in first:
             copy.wait()
 
         def ready():
+            for copy in weights:
+                copy.wait()
+            fetched.extend(begin(far[k], close[k], later_sems.at[k]) for k in range(count))
             for ky in range(3):
-                weights[ky].wait()
                 taps[pl.ds(ky * C, C)] = jnp.concatenate([kernel[ky, kx] for kx in range(3)], axis=1)
 
         enc_rest(current, gain_near, beta_near, bias_near, taps, wide, sums, send, ready)
@@ -208,20 +210,24 @@
     return lax.dot_general(wide[...], taps[...], (((1,), (1,)), ((), ())), preferred_element_type=F32)
 
 
-def dec_first(current, skips, kernel, dec_rows, enc_sent):
-    def body(current, skips, kernel, bias, gain, beta, early, send, near, far, encoded, *scratch):
-        wide, sums, result, sems = scratch
-        taps = (near, far)
+def dec_first(current, skips, weight, dec_rows, enc_sent):
+    def body(current, skips, weight, bias, gain, beta, early, send, near, far, encoded, *scratch):
+        kernel, wide, sums, result, sems = scratch
+        weights = [begin(weight.at[ky], kernel.at[ky], sems.at[IMAGES + ky]) for ky in range(3)]
         copies = write_maps(early, result, encoded, sems, 0, 0)
-        loads = [lambda m=m, i=i: m[image(i)] for m in (current, skips) for i in range(IMAGES)]
+        starts = ((current, 0), (skips, 0))
+        loads = [lambda m=m, i=i, base=base: m[image(i, base)] for m, base in starts for i in range(IMAGES)]
         gains = [gain[:, :C]] * IMAGES + [gain[:, C:]] * IMAGES
         betas = [beta[:, :C]] * IMAGES + [beta[:, C:]] * IMAGES
         hidden = norm_all(loads, gains, betas, 2 * C // GROUPS)
-        for part in range(2):
+        for source in range(2):
             for i in range(IMAGES):
-                wide[part, image(i)] = spread_rows(hidden[part * IMAGES + i])
-            cut = slice(part * C, (part + 1) * C)
-            taps[part][...] = jnp.concatenate([kernel[ky, :, cut] for ky in range(3)], axis=1)
+                wide[source, image(i)] = spread_rows(hidden[source * IMAGES + i])
+        for copy in weights:
+            copy.wait()
+        for half, taps in enumerate((near, far)):
+            cut = slice(half * C, (half + 1) * C)
+            taps[...] = jnp.concatenate([kernel[ky, :, cut] for ky in range(3)], axis=1)
         sums[...] = multiply(wide.at[0], near) + multiply(wide.at[1], far)
         for i in range(IMAGES):
             total = current[image(i)].astype(F32) + gather_columns(sums[image(i)]) + bias[...]
@@ -231,14 +237,20 @@
 
     return call(
         body,
-        (current, skips, kernel) + tuple(dec_rows) + (enc_sent,),
-        [VMEM] * 7,
-        [pltpu.VMEM(PARCEL, BF16), pltpu.VMEM((TAPS, TAPS), BF16), pltpu.VMEM((TAPS, TAPS), BF16), WHOLE],
-        [
+        (current, skips, weight) + tuple(dec_rows) + (enc_sent,),
+        [VMEM, VMEM, HBM] + [VMEM] * 4,
+        [
+            pltpu.VMEM(PARCEL, BF16),
+            pltpu.VMEM((TAPS, TAPS), BF16),
+            pltpu.VMEM((TAPS, TAPS), BF16),
+            WHOLE,
+        ],
+        [
+            pltpu.VMEM((3, TAPS, 2 * C), BF16),
             pltpu.VMEM((2, ROWS, TAPS), BF16),
             pltpu.VMEM((ROWS, TAPS), F32),
             pltpu.VMEM((ROWS, C), BF16),
-            pltpu.SemaphoreType.DMA((IMAGES,)),
+            pltpu.SemaphoreType.DMA((IMAGES + 3,)),
         ],
     )
 
@@ -311,11 +323,12 @@
     )[0]
 
 
-def queue_maps(turned, moved, last):
-    def body(turned, moved, last, out, chosen, result, sems):
+def queue_maps(direct, turned, moved, last):
+    def body(direct, turned, moved, last, out, chosen, result, sems):
         shared = lax.axis_index("section") % 4 == 0
-        for i in range(IMAGES):
-            chosen[i] = jnp.where(shared, moved[i], turned[i])
+        first = lax.axis_index("dp") % 2 == 0
+        for i in range(IMAGES):
+            chosen[i] = jnp.where(shared, moved[i], jnp.where(first, direct[i], turned[i]))
         copies = write_maps(chosen, result, out, sems, 0, 0)
         copies += write_maps(last, result, out, sems, ROWS, 1)
         for copy in copies:
@@ -323,8 +336,8 @@
 
     return call(
         body,
-        (turned, moved, last),
-        [VMEM, VMEM, VMEM],
+        (direct, turned, moved, last),
+        [VMEM, VMEM, VMEM, VMEM],
         [WHOLE],
         [
             pltpu.VMEM(PARCEL, BF16),
@@ -350,13 +363,14 @@
 ):
     forward = [(s, (s + 1) % 8) for s in range(8)]
     mirror = [(s, 7 - s) for s in range(8)]
-    relay = [(s, 8 - s) for s in range(1, 8) if s != 4]
+    groups = lax.axis_size("dp")
+    direct = [(groups * s + g, groups * (7 - s) + g) for g in range(0, groups, 2) for s in range(8) if s % 4 != 3]
+    relay = [(groups * s + g, groups * (8 - s) + g) for g in range(1, groups, 2) for s in range(8) if s % 4]
     enc_kernel = enc_weight.reshape(3, 3, C, C)
     dec_kernel = jnp.transpose(dec_weight, (0, 1, 2, 4, 3)).reshape(3, TAPS, 2 * C)
     later = (
         dec_in.reshape(ROWS, C),
         skip_queue.reshape(TICKS * ROWS, C),
-        dec_kernel,
         dec_bias,
         dec_gain,
         dec_beta,
@@ -365,16 +379,17 @@
     enc_sent, enc_taps, *held = enc_first(
         enc_in.reshape(ROWS, C), enc_kernel, (enc_bias, enc_gain, enc_beta), later
     )
-    enc_rows, (dec_now, skips, dec_kernel), dec_rows, fresh_now = held[:3], held[3:6], held[6:9], held[9]
+    enc_rows, (dec_now, skips), dec_rows, fresh_now = held[:3], held[3:5], held[5:8], held[8]
     moved_enc = lax.ppermute(enc_sent, "section", forward)
-    dec_sent, dec_taps, skip_taps, encoded = dec_first(dec_now, skips, dec_kernel, dec_rows, enc_sent)
+    turned_direct = lax.ppermute(enc_sent, ("section", "dp"), direct)
+    dec_sent, near, far, encoded = dec_first(dec_now, skips, dec_kernel, dec_rows, enc_sent)
+    turned = lax.ppermute(moved_enc, ("section", "dp"), relay)
     moved_dec = lax.ppermute(dec_sent, "section", [pair for pair in forward if pair[1] != 0])
-    turned = lax.ppermute(moved_enc, "section", relay)
     last_sent, decoded = enc_second(fresh_now, moved_enc, enc_taps, enc_rows, dec_sent)
     last = lax.ppermute(last_sent, "section", mirror)
-    part, encoded = dec_skip(moved_enc, skips, skip_taps, dec_rows, last_sent, encoded)
-    decoded = dec_second(moved_enc, moved_dec, dec_taps, part, dec_rows, decoded)
-    queued = queue_maps(turned, moved_enc, last)
+    part, encoded = dec_skip(moved_enc, skips, far, dec_rows, last_sent, encoded)
+    decoded = dec_second(moved_enc, moved_dec, near, part, dec_rows, decoded)
+    queued = queue_maps(turned_direct, turned, moved_enc, last)
     shape = (TICKS * IMAGES, SIDE, SIDE, C)
     return encoded.reshape(shape), decoded.reshape(shape), queued.reshape(shape)
 

time: 40 us -> 36.5 us (0.912)
  waiting for transfers between devices: 9.88 us -> 6.09 us
  starting transfers between devices: 10.6 us -> 11.3 us
    ppermute x1, waiting for transfers between devices: 7.27 us -> 3.52 us  [shards(): last = lax.ppermute(last_sent, 'section', mirror)]
    ppermute x1, waiting for transfers between devices: 0.01 us -> 2.56 us  [shards(): lax.ppermute(dec_sent, 'section', [pair for pair in forward if pair[1] !=...]
    ppermute x1 -> x2, starting transfers between devices: 2.89 us -> 4.42 us  [the longest x1 3.57 us: shards(): turned_direct = lax.ppermute(enc_sent, ('section', 'dp'), direct)]
    ppermute x1, waiting for transfers between devices: 1.5 us -> 0.01 us  [shards(): moved_enc = lax.ppermute(enc_sent, 'section', forward)]
    ppermute x1 -> x2, waiting for transfers between devices: 1.1 us -> 0.01 us  [the longest x1 0.01 us: shards(): turned = lax.ppermute(moved_enc, ('section', 'dp'), relay)]
    ppermute x1, starting transfers between devices: 2.95 us -> 1.92 us  [shards(): lax.ppermute(dec_sent, 'section', [pair for pair in forward if pair[1] !=...]
  transfers between devices with their start and end apart: 4 -> 5, of which waited for: 3 -> 2; matrix products, arithmetic and copies ran while one was open for 0% -> 0% of each run, Pallas kernels for 30% -> 37%
where the time goes in v4:
time: 36.5 us; the launch traced here: 36 us
  Pallas kernels  17.8 us (49%)
  starting transfers between devices  11.3 us (31%)
  waiting for transfers between devices  6.09 us (17%)
  between operations  0.88 us (2%)
    pallas_call x6, Pallas kernels, call(): pl.pallas_call(body, out_shape=tuple(outputs), in_specs=list(in_specs), o...  17.8 us
    ppermute x1, starting transfers between devices, shards(): turned_direct = lax.ppermute(enc_sent, ('section', 'dp'), direct)  3.57 us
    ppermute x1, waiting for transfers between devices, shards(): last = lax.ppermute(last_sent, 'section', mirror)  3.52 us
    ppermute x1, starting transfers between devices, shards(): last = lax.ppermute(last_sent, 'section', mirror)  2.94 us
    ppermute x1, waiting for transfers between devices, shards(): lax.ppermute(dec_sent, 'section', [pair for pair in forward if pair[1] !=...  2.56 us
    ppermute x1, starting transfers between devices, shards(): moved_enc = lax.ppermute(enc_sent, 'section', forward)  1.99 us
    ppermute x1, starting transfers between devices, shards(): lax.ppermute(dec_sent, 'section', [pair for pair in forward if pair[1] !=...  1.92 us
    ppermute x1, starting transfers between devices, shards(): turned = lax.ppermute(moved_enc, ('section', 'dp'), relay)  0.85 us
  transfers between devices with their start and end apart: 5, of which 2 were waited for; matrix products, arithmetic and copies ran while one was open for 0% of the time, Pallas kernels for 37%

profile of v4, /device:TPU:82, one launch (start us, length us, event | category | flops | bytes accessed | tf_op | source)
XLA Modules:
  0.0 36.0 jit_solution(15725831009246476677)
XLA Ops:
  0.6 3.6 %shard_map.139 = (bf16[2,128,640]{2,1,0:T(8,128)(2,1)S(1)}, bf16[960,960]{1,0:T(8,128)(2,1)S(1)}, f32[1,320]{1,0:T(1,128)S(1)}, f32[1,320]{1,0:T(1,128)S(1)}, f3...) custom-call(bf16[512,320]{1,0:T(8,128)(2,1)} %bitcast.17, ...), custom_call_target="tpu_custom_call" | custom-call | tf_op jit(solution)/shard_map/pallas_call | solution.py:103
  4.2 2.0 %collective-permute-start = (bf16[2,128,640]{2,1,0:T(8,128)(2,1)S(1)}, bf16[2,128,640]{2,1,0:T(8,128)(2,1)S(1)}, u32[]{:S(2)}, u32[]{:S(2)}) collective-permute-start(bf16[2,128,640]{2,1,0:T(8,128)(2,1)S(1)} %get-tuple-element.22.early), channel_id=1, source_target_pairs={{0,32},{32,64},{64,96},{96,128},{128,160},{160,192},{192,224},{224... | collective-permute-start | bytes 983048 | tf_op jit(solution)/shard_map/ppermute | solution.py:383
  6.2 3.6 %collective-permute-start.2 = (bf16[2,128,640]{2,1,0:T(8,128)(2,1)S(1)}, bf16[2,128,640]{2,1,0:T(8,128)(2,1)S(1)}, u32[]{:S(2)}, u32[]{:S(2)}) collective-permute-start(bf16[2,128,640]{2,1,0:T(8,128)(2,1)S(1)} %get-tuple-element.22.early), channel_id=1, source_target_pairs={{0,224},{32,192},{64,160},{128,96},{160,64},{192,32},{2,226},{34,1... | collective-permute-start | bytes 983048 | tf_op jit(solution)/shard_map/ppermute | solution.py:384
  9.8 5.2 %shard_map.140 = (bf16[2,128,640]{2,1,0:T(8,128)(2,1)S(1)}, bf16[960,960]{1,0:T(8,128)(2,1)S(1)}, bf16[960,960]{1,0:T(8,128)(2,1)S(1)}, bf16[1024,320]{1,0:T(8,128)(2,1)}) custom-call(bf16[512,320]{1,0:T(8,128)(2,1)S(1)} %get-tuple-element.24.current, bf16[1024,320]{1,0:T(8,128)(2,1)S(1)} %get-tuple-element.23.skips, bf16[3,960,640]{2,1,0:T(8,128)(2,1)} %bitcast.11, ...), custom_call_target="tpu_custom_call" | custom-call | tf_op jit(solution)/shard_map/pallas_call | solution.py:103
  15.0 1.9 %collective-permute-start.1 = (bf16[2,128,640]{2,1,0:T(8,128)(2,1)S(1)}, bf16[2,128,640]{2,1,0:T(8,128)(2,1)S(1)}, u32[]{:S(2)}, u32[]{:S(2)}) collective-permute-start(bf16[2,128,640]{2,1,0:T(8,128)(2,1)S(1)} %get-tuple-element.34.early), channel_id=1, source_target_pairs={{0,32},{32,64},{64,96},{96,128},{128,160},{160,192},{192,224},{1,3... | collective-permute-start | bytes 983048 | tf_op jit(solution)/shard_map/ppermute | solution.py:387
  16.9 0.0 collective-permute-done.moved.moved_enc
  16.9 2.5 %shard_map.141 = (bf16[2,128,640]{2,1,0:T(8,128)(2,1)S(1)}, bf16[1024,320]{1,0:T(8,128)(2,1)}) custom-call(bf16[512,320]{1,0:T(8,128)(2,1)S(1)} %get-tuple-element.29.fresh, bf16[2,128,640]{2,1,0:T(8,128)(2,1)S(1)} %collective-permute-done.moved.moved_enc, bf16[960,960]{1,0:T(8,128)(2,1)S(1)} %get-tuple-element.30.taps, ...), custom_call_target="tpu_custom_call" | custom-call | tf_op jit(solution)/shard_map/pallas_call | solution.py:103
  19.4 2.9 %collective-permute-start.4 = (bf16[2,128,640]{2,1,0:T(8,128)(2,1)S(1)}, bf16[2,128,640]{2,1,0:T(8,128)(2,1)S(1)}, u32[]{:S(2)}, u32[]{:S(2)}) collective-permute-start(bf16[2,128,640]{2,1,0:T(8,128)(2,1)S(1)} %get-tuple-element.35.late), channel_id=1, source_target_pairs={{0,224},{32,192},{64,160},{96,128},{128,96},{160,64},{192,32},{224... | collective-permute-start | bytes 983048 | tf_op jit(solution)/shard_map/ppermute | solution.py:389
  22.4 0.8 %collective-permute-start.3 = (bf16[2,128,640]{2,1,0:T(8,128)(2,1)S(1)}, bf16[2,128,640]{2,1,0:T(8,128)(2,1)S(1)}, u32[]{:S(2)}, u32[]{:S(2)}) collective-permute-start(bf16[2,128,640]{2,1,0:T(8,128)(2,1)S(1)} %collective-permute-done.moved.moved_enc), channel_id=1, source_target_pairs={{33,225},{65,193},{97,161},{161,97},{193,65},{225,33},{35,227},{67... | collective-permute-start | bytes 983048 | tf_op jit(solution)/shard_map/ppermute | solution.py:386
  23.2 2.6 %shard_map.142 = (f32[512,320]{1,0:T(8,128)S(1)}, bf16[1024,320]{1,0:T(8,128)(2,1)}) custom-call(bf16[2,128,640]{2,1,0:T(8,128)(2,1)S(1)} %collective-permute-done.moved.moved_enc, bf16[1024,320]{1,0:T(8,128)(2,1)S(1)} %get-tuple-element.23.skips, bf16[960,960]{1,0:T(8,128)(2,1)S(1)} %get-tuple-element.28.taps, ...), custom_call_target="tpu_custom_call", output_to_operand_aliasing={{1}: (7, {})} | custom-call | tf_op jit(solution)/shard_map/pallas_call | solution.py:103
  25.8 2.6 %collective-permute-done.1.moved_dec = bf16[2,128,640]{2,1,0:T(8,128)(2,1)S(1)} collective-permute-done((bf16[2,128,640]{2,1,0:T(8,128)(2,1)S(1)}, bf16[2,128,640]{2,1,0:T(8,128)(2,1)S(1)}, u32[]{:S(2)}, u32[]{:S(2)}) %collective-permute-start.1) | collective-permute-done | bytes 327712 | tf_op jit(solution)/shard_map/ppermute | solution.py:387
  28.3 2.9 %shard_map.143 = bf16[1024,320]{1,0:T(8,128)(2,1)} custom-call(bf16[2,128,640]{2,1,0:T(8,128)(2,1)S(1)} %collective-permute-done.moved.moved_enc, bf16[2,128,640]{2,1,0:T(8,128)(2,1)S(1)} %collective-permute-done.1.moved_dec, bf16[960,960]{1,0:T(8,128)(2,1)S(1)} %get-tuple-element.38.taps, ...), custom_call_target="tpu_custom_call", output_to_operand_aliasing={{}: (6, {})} | custom-call | tf_op jit(solution)/shard_map/pallas_call | solution.py:103
  31.3 0.0 collective-permute-done.2.direct
  31.3 3.5 %collective-permute-done.4.last = bf16[2,128,640]{2,1,0:T(8,128)(2,1)S(1)} collective-permute-done((bf16[2,128,640]{2,1,0:T(8,128)(2,1)S(1)}, bf16[2,128,640]{2,1,0:T(8,128)(2,1)S(1)}, u32[]{:S(2)}, u32[]{:S(2)}) %collective-permute-start.4) | collective-permute-done | bytes 327712 | tf_op jit(solution)/shard_map/ppermute | solution.py:389
  34.8 0.0 collective-permute-done.3.turned
  34.8 1.0 %shard_map.144 = bf16[1024,320]{1,0:T(8,128)(2,1)} custom-call(bf16[2,128,640]{2,1,0:T(8,128)(2,1)S(1)} %collective-permute-done.2.direct, bf16[2,128,640]{2,1,0:T(8,128)(2,1)S(1)} %collective-permute-done.3.turned, bf16[2,128,640]{2,1,0:T(8,128)(2,1)S(1)} %collective-permute-done.moved.moved_enc, bf16[2,128,640]{2,1,0:T(8,128)(2,1)S(1)} %collective-permute-done.4.last), custom_call_target="tpu_custom_call" | custom-call | tf_op jit(solution)/shard_map/pallas_call | solution.py:103
Async XLA Ops:
  4.2 12.7 %collective-permute-start = (bf16[2,128,640]{2,1,0:T(8,128)(2,1)S(1)}, bf16[2,128,640]{2,1,0:T(8,128)(2,1)S(1)}, u32[]{:S(2)}, u32[]{:S(2)}) collective-permute-start(bf16[2,128,640]{2,1,0:T(8,128)(2,1)S(1)} %get-tuple-element.22.early), channel_id=1, source_target_pairs={{0,32},{32,64},{64,96},{96,128},{128,160},{160,192},{192,224},{224... | collective-permute-start | bytes 983048 | tf_op jit(solution)/shard_map/ppermute | solution.py:383
  6.2 25.1 %collective-permute-start.2 = (bf16[2,128,640]{2,1,0:T(8,128)(2,1)S(1)}, bf16[2,128,640]{2,1,0:T(8,128)(2,1)S(1)}, u32[]{:S(2)}, u32[]{:S(2)}) collective-permute-start(bf16[2,128,640]{2,1,0:T(8,128)(2,1)S(1)} %get-tuple-element.22.early), channel_id=1, source_target_pairs={{0,224},{32,192},{64,160},{128,96},{160,64},{192,32},{2,226},{34,1... | collective-permute-start | bytes 983048 | tf_op jit(solution)/shard_map/ppermute | solution.py:384
  15.0 13.4 %collective-permute-start.1 = (bf16[2,128,640]{2,1,0:T(8,128)(2,1)S(1)}, bf16[2,128,640]{2,1,0:T(8,128)(2,1)S(1)}, u32[]{:S(2)}, u32[]{:S(2)}) collective-permute-start(bf16[2,128,640]{2,1,0:T(8,128)(2,1)S(1)} %get-tuple-element.34.early), channel_id=1, source_target_pairs={{0,32},{32,64},{64,96},{96,128},{128,160},{160,192},{192,224},{1,3... | collective-permute-start | bytes 983048 | tf_op jit(solution)/shard_map/ppermute | solution.py:387
  19.4 15.4 %collective-permute-start.4 = (bf16[2,128,640]{2,1,0:T(8,128)(2,1)S(1)}, bf16[2,128,640]{2,1,0:T(8,128)(2,1)S(1)}, u32[]{:S(2)}, u32[]{:S(2)}) collective-permute-start(bf16[2,128,640]{2,1,0:T(8,128)(2,1)S(1)} %get-tuple-element.35.late), channel_id=1, source_target_pairs={{0,224},{32,192},{64,160},{96,128},{128,96},{160,64},{192,32},{224... | collective-permute-start | bytes 983048 | tf_op jit(solution)/shard_map/ppermute | solution.py:389
  22.4 12.4 %collective-permute-start.3 = (bf16[2,128,640]{2,1,0:T(8,128)(2,1)S(1)}, bf16[2,128,640]{2,1,0:T(8,128)(2,1)S(1)}, u32[]{:S(2)}, u32[]{:S(2)}) collective-permute-start(bf16[2,128,640]{2,1,0:T(8,128)(2,1)S(1)} %collective-permute-done.moved.moved_enc), channel_id=1, source_target_pairs={{33,225},{65,193},{97,161},{161,97},{193,65},{225,33},{35,227},{67... | collective-permute-start | bytes 983048 | tf_op jit(solution)/shard_map/ppermute | solution.py:386
